TPU v7x, 128 devices: a whole 4x4x4 slice. The times are simulated.
128 devices in a mesh: dp: 16 (over y, z_lo, core), freq: 8 (over x, z_hi).
Axes of the slice: x: 4, y: 4, z: 4 (z_hi: 2, z_lo: 2; z = z_hi * 2 + z_lo), core: 2. Of those that a mesh axis runs over, the one named last changes fastest.
Arguments:
- records: float32 [16, 2, 1024, 2048], P('dp', None, None, 'freq'), may hold values from -6 to 6
- stem_weight: bfloat16 [256, 512], replicated, may hold values from -0.375 to 0.375
- conv_weight: bfloat16 [3, 3, 16, 512], replicated, may hold values from -0.875 to 0.875
- mix_weight: bfloat16 [3, 512, 512], replicated, may hold values from -0.25 to 0.25
- head_weight: float32 [512, 10], replicated, may hold values from -0.25 to 0.25
- labels: int32 [16], P('dp'), may hold values from 0 to 9
- band_bounds: int32 [33], replicated, may hold values from 0 to 1048576, as said below
Outputs:
- loss: float32 [], replicated
- grad_stem: float32 [256, 512], replicated
- grad_conv: float32 [3, 3, 16, 512], replicated
- grad_mix: float32 [3, 512, 512], replicated
- grad_head: float32 [512, 10], replicated
Inputs may be any that keep to these rules, and one draw needn't show every extreme that they name: `band_bounds`: strictly increasing multiples of 128; the first is 0 and the last is half of 2097152.
All inputs are finite; a program needn't handle non-finite values.
Results may differ from a plain program's by a relative error of at most 0.0018.
Values may be sent and summed in bfloat16 or wider, within the bound.
A program may use at most 128 MiB of HBM per device.

v0:
```python
import jax
import jax.numpy as jnp
from jax import lax
from jax.sharding import PartitionSpec as P

POOL = 128
GROUP_WIDTH = 16
KW = 3


EXACT_DOTS = lax.Precision.HIGHEST
EPS = 1e-05


def with_halo(x, sides, width):
    for axis, dim in sides:
        devices, length = (lax.axis_size(axis), x.shape[dim])
        up = [(i, (i + 1) % devices) for i in range(devices - 1)]
        down = [(j, i) for i, j in up]
        last = lax.slice_in_dim(x, length - width, length, axis=dim)
        first = lax.slice_in_dim(x, 0, width, axis=dim)
        before = lax.ppermute(last, axis, up)
        after = lax.ppermute(first, axis, down)
        x = jnp.concatenate([before, x, after], axis=dim)
    return x


def from_partner(x, axis, stride):
    return lax.ppermute(x, axis, [(i, i ^ 1 << stride) for i in range(lax.axis_size(axis))])


def first_section(signal, imaginary):
    table_size = signal.shape[-2]
    row_index = lax.broadcasted_iota(jnp.int32, (table_size, table_size), 0)
    col_index = lax.broadcasted_iota(jnp.int32, (table_size, table_size), 1)
    angles = (col_index * (2 * row_index + 1) % (2 * table_size)).astype(jnp.float32) * (
        jnp.pi / table_size
    )
    cosine_table = jnp.cos(angles)
    sine_table = jnp.sin(angles)

    def table_product(table, values):
        return jnp.einsum("kn,...nm->...km", table, values, precision=EXACT_DOTS)

    real_part = table_product(cosine_table, signal) + table_product(sine_table, imaginary)
    imag_part = table_product(cosine_table, imaginary) - table_product(sine_table, signal)
    return (real_part, imag_part)


def apply_twiddle(real_part, imag_part, offset, total_len):
    row_count = real_part.shape[-2]
    col_count = real_part.shape[-1]
    row_index = lax.broadcasted_iota(jnp.int32, (row_count, col_count), 0)
    col_index = lax.broadcasted_iota(jnp.int32, (row_count, col_count), 1) + offset
    angles = (col_index * (2 * row_index + 1) % (2 * total_len)).astype(jnp.float32) * (
        jnp.pi / total_len
    )
    cosine_table = jnp.cos(angles)
    sine_table = jnp.sin(angles)
    return (
        real_part * cosine_table + imag_part * sine_table,
        imag_part * cosine_table - real_part * sine_table,
    )


def second_section(real_part, imag_part, columns):
    length = real_part.shape[-1]
    block_width = min(columns, 512)
    row_index = lax.broadcasted_iota(jnp.int32, (length, block_width), 0)

    def table_product(values, table):
        return jnp.einsum("...n,nc->...c", values, table, precision=EXACT_DOTS)

    def one_block(block_idx):
        col_index = (
            lax.broadcasted_iota(jnp.int32, (length, block_width), 1) + block_idx * block_width
        )
        angles = (row_index * col_index % length).astype(jnp.float32) * (2.0 * jnp.pi / length)
        cosine_table = jnp.cos(angles)
        sine_table = jnp.sin(angles)
        real_out = table_product(real_part, cosine_table) + table_product(imag_part, sine_table)
        imag_out = table_product(imag_part, cosine_table) - table_product(real_part, sine_table)
        return jnp.stack([real_out, imag_out])

    blocks = lax.map(one_block, jnp.arange(columns // block_width))
    blocks = jnp.moveaxis(blocks, 0, -2)
    return blocks.reshape(blocks.shape[:-2] + (columns,))


def finish_packed(exchanged):
    return second_section(exchanged[:, 0], exchanged[:, 1], exchanged.shape[-1])


def bin_features(power, total_len):
    return jnp.swapaxes(jnp.log1p(power / total_len), 1, 2).astype(jnp.bfloat16)


def with_edges(values):
    return with_halo(values, (("freq", 1),), 1)


def group_mask(channels):
    row_group = lax.broadcasted_iota(jnp.int32, (channels, channels), 0) // GROUP_WIDTH
    col_group = lax.broadcasted_iota(jnp.int32, (channels, channels), 1) // GROUP_WIDTH
    return row_group == col_group


def dense_taps(tap_weights):
    channels = tap_weights.shape[-1]
    groups = channels // GROUP_WIDTH
    tiled = jnp.tile(tap_weights, (1, groups, 1))
    return jnp.where(group_mask(channels)[None], tiled, jnp.zeros_like(tiled))


def conv_forward(padded, dense_kernel, span_len):
    result = None
    for tap_idx in range(KW):
        window = padded[:, tap_idx : tap_idx + span_len]
        term = jnp.einsum(
            "rpc,cd->rpd", window, dense_kernel[tap_idx], preferred_element_type=jnp.float32
        )
        result = term if result is None else result + term
    return result


def conv_backward(grad_padded, dense_kernel, span_len):
    result = None
    for tap_idx in range(KW):
        shift_at = KW - 1 - tap_idx
        window = grad_padded[:, shift_at : shift_at + span_len]
        term = jnp.einsum(
            "rpd,cd->rpc", window, dense_kernel[tap_idx], preferred_element_type=jnp.float32
        )
        result = term if result is None else result + term
    return result


def conv_weight_grad(padded, grad_pre, span_len):
    channels = padded.shape[-1]
    groups = channels // GROUP_WIDTH
    picker = group_mask(channels).astype(jnp.float32).reshape(groups, GROUP_WIDTH, channels)[:, :1]
    tap_list = []
    for tap_idx in range(KW):
        window = padded[:, tap_idx : tap_idx + span_len]
        full_grad = jnp.einsum("rpc,rpd->cd", window, grad_pre, preferred_element_type=jnp.float32)
        tap_list.append(jnp.sum(full_grad.reshape(groups, GROUP_WIDTH, channels) * picker, axis=0))
    return jnp.stack(tap_list)


def local(records, stem_weight, conv_weight, mix_weight, head_weight, labels, band_bounds):
    freq_size = lax.axis_size("freq")
    my_place = lax.axis_index("freq")
    record_count = records.shape[0]
    first_len = records.shape[2]
    local_cols = records.shape[3]
    total_len = first_len * local_cols * freq_size
    col_offset = my_place * local_cols
    half_cols = local_cols * freq_size // 2
    real_part, imag_part = first_section(records[:, 0], records[:, 1])
    real_part, imag_part = apply_twiddle(real_part, imag_part, col_offset, total_len)
    stacked = jnp.stack([real_part, imag_part], axis=1)
    spectrum = finish_packed(
        lax.all_to_all(stacked, "freq", split_axis=2, concat_axis=3, tiled=True)
    )
    upper_half = spectrum[..., half_cols:]
    for bit_idx in range(freq_size.bit_length() - 1):
        upper_half = from_partner(upper_half, "freq", bit_idx)
    mirrored = upper_half[..., ::-1, ::-1]
    z_real = spectrum[0, ..., :half_cols]
    z_imag = spectrum[1, ..., :half_cols]
    m_real = mirrored[0]
    m_imag = mirrored[1]
    power_a = ((z_real + m_real) ** 2 + (z_imag - m_imag) ** 2) * 0.25
    power_b = ((z_imag + m_imag) ** 2 + (z_real - m_real) ** 2) * 0.25
    feat_a = bin_features(power_a, total_len)
    feat_b = bin_features(power_b, total_len)
    exchanged = (
        lax.all_to_all(feat_a, "freq", split_axis=1, concat_axis=2, tiled=True),
        lax.all_to_all(feat_b, "freq", split_axis=1, concat_axis=2, tiled=True),
    )
    pieces = []
    for values in exchanged:
        pieces.append(values.reshape(values.shape[0], -1, POOL))
    positions = jnp.concatenate(pieces, axis=-1)
    stream = jnp.einsum("rpf,fc->rpc", positions, stem_weight, preferred_element_type=jnp.float32)
    local_len = stream.shape[1]
    channels = stream.shape[2]
    groups = channels // GROUP_WIDTH
    layer_count = conv_weight.shape[0]
    saved_layers = []
    for layer_idx in range(layer_count):
        dense_kernel = dense_taps(conv_weight[layer_idx])
        scales = lax.rsqrt(jnp.mean(stream * stream, axis=-1, keepdims=True) + EPS)
        normed = (stream * scales).astype(jnp.bfloat16)
        padded = with_edges(normed)
        preact = conv_forward(padded, dense_kernel, local_len)
        activated = jax.nn.silu(preact).astype(jnp.bfloat16)
        saved_layers.append((stream, padded, preact, activated, dense_kernel))
        stream = stream + jnp.einsum(
            "rpc,cd->rpd", activated, mix_weight[layer_idx], preferred_element_type=jnp.float32
        )
    starts = (my_place * local_len + lax.broadcasted_iota(jnp.int32, (local_len, 1), 0)) * POOL
    member = ((starts >= band_bounds[None, :-1]) & (starts < band_bounds[None, 1:])).astype(
        jnp.float32
    )
    counts = ((band_bounds[1:] - band_bounds[:-1]) // POOL).astype(jnp.float32)
    partial_value = jnp.einsum(
        "pg,rpgo->rgo",
        member,
        stream.reshape(record_count, local_len, groups, GROUP_WIDTH),
        precision=EXACT_DOTS,
    )
    band_sum = lax.psum(partial_value, "freq")
    pooled = (band_sum / counts[:, None]).reshape(record_count, channels)
    logits = jnp.dot(pooled, head_weight, precision=EXACT_DOTS)
    exponents = jnp.exp(logits)
    denominator = jnp.sum(exponents, axis=-1, keepdims=True)
    one_hot = (
        labels[:, None] == lax.broadcasted_iota(jnp.int32, (1, head_weight.shape[1]), 1)
    ).astype(jnp.float32)
    all_records = record_count * lax.axis_size("dp")
    lead_flag = (my_place == 0).astype(jnp.float32)
    loss_part = (
        jnp.sum(jnp.log(denominator[:, 0]) - jnp.sum(one_hot * logits, axis=-1))
        / all_records
        * lead_flag
    )
    grad_logits = (exponents / denominator - one_hot) / all_records
    head_part = jnp.dot(pooled.T, grad_logits, precision=EXACT_DOTS) * lead_flag
    grad_band = (
        jnp.dot(grad_logits, head_weight.T, precision=EXACT_DOTS).reshape(
            record_count, groups, GROUP_WIDTH
        )
        / counts[:, None]
    )
    grad_stream = (member[None, :, :, None] * grad_band[:, None]).reshape(
        record_count, local_len, channels
    )
    conv_grads = [None] * layer_count
    mix_grads = [None] * layer_count
    for layer_idx in reversed(range(layer_count)):
        stream_in, padded, preact, activated, dense_kernel = saved_layers[layer_idx]
        grad_out = grad_stream.astype(jnp.bfloat16)
        mix_grad = jnp.einsum(
            "rpc,rpd->cd", activated, grad_out, preferred_element_type=jnp.float32
        )
        grad_act = jnp.einsum(
            "rpd,cd->rpc", grad_out, mix_weight[layer_idx], preferred_element_type=jnp.float32
        )
        gate_value = jax.nn.sigmoid(preact)
        grad_pre = (grad_act * gate_value * (1.0 + preact * (1.0 - gate_value))).astype(
            jnp.bfloat16
        )
        grad_padded = with_edges(grad_pre)
        grad_normed = conv_backward(grad_padded, dense_kernel, local_len)
        tap_grads = conv_weight_grad(padded, grad_pre, local_len)
        conv_grads[layer_idx] = tap_grads
        mix_grads[layer_idx] = mix_grad
        scales = lax.rsqrt(jnp.mean(stream_in * stream_in, axis=-1, keepdims=True) + EPS)
        grad_stream = (
            grad_stream
            + scales * grad_normed
            - stream_in * scales**3 * jnp.mean(stream_in * grad_normed, axis=-1, keepdims=True)
        )
    grad_stem = jnp.einsum(
        "rpf,rpc->fc", positions.astype(jnp.float32), grad_stream, precision=EXACT_DOTS
    )
    loss_all, stem_all, conv_all, mix_all, head_all = lax.psum(
        (loss_part, grad_stem, jnp.stack(conv_grads), jnp.stack(mix_grads), head_part),
        ("dp", "freq"),
    )
    return (loss_all, stem_all, conv_all, mix_all, head_all)


def solution(mesh):
    in_specs = (P("dp", None, None, "freq"), P(), P(), P(), P(), P("dp"), P())
    out_specs = (P(), P(), P(), P(), P())
    return jax.shard_map(local, mesh=mesh, in_specs=in_specs, out_specs=out_specs, check_vma=False)
```

profile of v0, /device:TPU:1, one launch (start us, length us, event | category | flops | bytes accessed | tf_op | source)
XLA Modules:
  0.0 1006.3 jit_solution(10993358660560208359)
XLA Ops:
  7.2 20.3 %fusion.67 = f32[1024,256]{1,0:T(8,128)S(1)} fusion(s32[1024]{0:T(1024)S(1)} %multiply_add_fusion.1, f32[1,2,1024,256]{3,2,1,0:T(8,128)} %param.9), kind=kOutput, calls=%fused_computation.91 | convolution fusion | flops 3235905536 | bytes 2101248 | tf_op jit(solution)/shard_map/kn,...nm->...km/dot_general | solution.py:43
  27.5 20.6 %fusion.65 = f32[1024,256]{1,0:T(8,128)} fusion(s32[1024]{0:T(1024)S(1)} %multiply_add_fusion.1, f32[1,2,1024,256]{3,2,1,0:T(8,128)S(1)} %copy-done.67), kind=kOutput, calls=%fused_computation.90 | convolution fusion | flops 3235905536 | bytes 2101248 | tf_op jit(solution)/shard_map/kn,...nm->...km/dot_general | solution.py:43
  48.1 19.2 %fusion.76 = f32[1,1024,256]{2,1,0:T(8,128)S(1)} fusion(f32[1024,256]{1,0:T(8,128)S(1)} %fusion.67, s32[1024]{0:T(1024)S(1)} %multiply_add_fusion.1, f32[1,2,1024,256]{3,2,1,0:T(8,128)S(1)} %copy-done.67), kind=kOutput, calls=%fused_computation.119 | convolution fusion | flops 3236167680 | bytes 3149824 | tf_op jit(solution)/shard_map/kn,...nm->...km/dot_general | solution.py:43
  67.3 28.4 %add_bitcast_fusion = (f32[1,1,1024,256]{3,2,1,0:T(8,128)S(1)}, f32[1,1,1024,256]{3,2,1,0:T(8,128)S(1)}) fusion(f32[1,1024,256]{2,1,0:T(8,128)S(1)} %fusion.76, s32[1024]{0:T(1024)S(1)} %multiply_add_fusion.1, s32[256]{0:T(256)S(1)} %iota_add_fusion.1, f32[1024,256]{1,0:T(8,128)} %fusion.65, f32[1,2,1024,256]{3,2,1,0:T(8,128)S(1)} %copy-done.67), kind=kOutput, calls=%fused_computation.198 | convolution fusion | flops 3241410560 | bytes 5252096 | tf_op jit(solution)/shard_map/kn,...nm->...km/dot_general | solution.py:43
  95.8 3.0 copy.83
  98.8 8.2 all-to-all-start
  107.0 30.6 %all-to-all-done = f32[1,2,1024,256]{3,1,0,2:T(2,128)S(1)} async-done(((f32[1,2,1024,256]{3,1,0,2:T(2,128)}), f32[1,2,1024,256]{3,1,0,2:T(2,128)S(1)}, u32[]{:S(2)}, u32[]{:S(2)}) %all-to-all-start) | async-done | bytes 2097184 | tf_op jit(solution)/shard_map/all_to_all | solution.py:163
  137.6 2.6 copy.84
  143.1 375.0 %while.13 = (s32[]{:T(128)}, f32[4,2,1,128,512]{3,4,0,1,2:T(8,128)}, s32[4]{0:T(128)S(1)}, f32[1,128,2048]{2,1,0:T(8,128)}, f32[1,128,2048]{2,1,0:T(8,128)S(1)}, /*index=5*/s32[]{:T(128)}, s32[1]{0:T(128)}) while((s32[]{:T(128)}, f32[4,2,1,128,512]{3,4,0,1,2:T(8,128)}, s32[4]{0:T(128)S(1)}, f32[1,128,2048]{2,1,0:T(8,128)}, ...), condition=%wide.region_1.2_spmd.clone, body=%wide.region_0.1_spmd.clone.sunk | while | flops 6501433856 | bytes 11020933 | solution.py:85
  144.5 23.0 %fusion.301 = f32[512,128]{1,0:T(8,128)S(1)} fusion(s32[512]{0:T(512)S(1)} %iota_add_fusion.3, f32[1,128,2048]{2,1,0:T(8,128)} %get-tuple-element.221), kind=kOutput, calls=%fused_computation.14.clone.1 | convolution fusion | flops 1625292800 | bytes 1312768 | tf_op jit(solution)/shard_map/while/body/eval_jaxpr/...n,nc->...c/dot_general | solution.py:72
  167.6 22.2 %fusion.302 = f32[1,1,128,512]{2,3,1,0:T(8,128)S(1)} fusion(f32[512,128]{1,0:T(8,128)S(1)} %fusion.301, s32[512]{0:T(512)S(1)} %iota_add_fusion.3, f32[1,128,2048]{2,1,0:T(8,128)S(1)} %get-tuple-element.222), kind=kOutput, calls=%fused_computation.18.clone.1 | convolution fusion | flops 1625358336 | bytes 1574912 | tf_op jit(solution)/shard_map/while/body/eval_jaxpr/...n,nc->...c/dot_general | solution.py:72
  189.8 22.2 %fusion.299 = f32[512,128]{1,0:T(8,128)S(1)} fusion(s32[512]{0:T(512)S(1)} %iota_add_fusion.3, f32[1,128,2048]{2,1,0:T(8,128)S(1)} %get-tuple-element.222), kind=kOutput, calls=%fused_computation.13.clone.1 | convolution fusion | flops 1625292800 | bytes 1312768 | tf_op jit(solution)/shard_map/while/body/eval_jaxpr/...n,nc->...c/dot_general | solution.py:72
  212.0 22.1 %fusion.300 = f32[1,1,128,512]{2,3,1,0:T(8,128)S(1)} fusion(f32[512,128]{1,0:T(8,128)S(1)} %fusion.299, s32[512]{0:T(512)S(1)} %iota_add_fusion.3, f32[1,128,2048]{2,1,0:T(8,128)S(1)} %copy-done.40), kind=kOutput, calls=%fused_computation.20.clone.1 | convolution fusion | flops 1625358336 | bytes 1574912 | tf_op jit(solution)/shard_map/while/body/eval_jaxpr/...n,nc->...c/dot_general | solution.py:72
  236.3 23.0 %fusion.301 = f32[512,128]{1,0:T(8,128)S(1)} fusion(s32[512]{0:T(512)S(1)} %iota_add_fusion.3, f32[1,128,2048]{2,1,0:T(8,128)} %get-tuple-element.221), kind=kOutput, calls=%fused_computation.14.clone.1 | convolution fusion | flops 1625292800 | bytes 1312768 | tf_op jit(solution)/shard_map/while/body/eval_jaxpr/...n,nc->...c/dot_general | solution.py:72
  259.4 22.4 %fusion.302 = f32[1,1,128,512]{2,3,1,0:T(8,128)S(1)} fusion(f32[512,128]{1,0:T(8,128)S(1)} %fusion.301, s32[512]{0:T(512)S(1)} %iota_add_fusion.3, f32[1,128,2048]{2,1,0:T(8,128)S(1)} %get-tuple-element.222), kind=kOutput, calls=%fused_computation.18.clone.1 | convolution fusion | flops 1625358336 | bytes 1574912 | tf_op jit(solution)/shard_map/while/body/eval_jaxpr/...n,nc->...c/dot_general | solution.py:72
  281.8 22.0 %fusion.299 = f32[512,128]{1,0:T(8,128)S(1)} fusion(s32[512]{0:T(512)S(1)} %iota_add_fusion.3, f32[1,128,2048]{2,1,0:T(8,128)S(1)} %get-tuple-element.222), kind=kOutput, calls=%fused_computation.13.clone.1 | convolution fusion | flops 1625292800 | bytes 1312768 | tf_op jit(solution)/shard_map/while/body/eval_jaxpr/...n,nc->...c/dot_general | solution.py:72
  303.7 22.1 %fusion.300 = f32[1,1,128,512]{2,3,1,0:T(8,128)S(1)} fusion(f32[512,128]{1,0:T(8,128)S(1)} %fusion.299, s32[512]{0:T(512)S(1)} %iota_add_fusion.3, f32[1,128,2048]{2,1,0:T(8,128)S(1)} %copy-done.40), kind=kOutput, calls=%fused_computation.20.clone.1 | convolution fusion | flops 1625358336 | bytes 1574912 | tf_op jit(solution)/shard_map/while/body/eval_jaxpr/...n,nc->...c/dot_general | solution.py:72
  328.3 23.0 %fusion.301 = f32[512,128]{1,0:T(8,128)S(1)} fusion(s32[512]{0:T(512)S(1)} %iota_add_fusion.3, f32[1,128,2048]{2,1,0:T(8,128)} %get-tuple-element.221), kind=kOutput, calls=%fused_computation.14.clone.1 | convolution fusion | flops 1625292800 | bytes 1312768 | tf_op jit(solution)/shard_map/while/body/eval_jaxpr/...n,nc->...c/dot_general | solution.py:72
  351.4 22.1 %fusion.302 = f32[1,1,128,512]{2,3,1,0:T(8,128)S(1)} fusion(f32[512,128]{1,0:T(8,128)S(1)} %fusion.301, s32[512]{0:T(512)S(1)} %iota_add_fusion.3, f32[1,128,2048]{2,1,0:T(8,128)S(1)} %get-tuple-element.222), kind=kOutput, calls=%fused_computation.18.clone.1 | convolution fusion | flops 1625358336 | bytes 1574912 | tf_op jit(solution)/shard_map/while/body/eval_jaxpr/...n,nc->...c/dot_general | solution.py:72
  373.5 22.0 %fusion.299 = f32[512,128]{1,0:T(8,128)S(1)} fusion(s32[512]{0:T(512)S(1)} %iota_add_fusion.3, f32[1,128,2048]{2,1,0:T(8,128)S(1)} %get-tuple-element.222), kind=kOutput, calls=%fused_computation.13.clone.1 | convolution fusion | flops 1625292800 | bytes 1312768 | tf_op jit(solution)/shard_map/while/body/eval_jaxpr/...n,nc->...c/dot_general | solution.py:72
  395.5 22.3 %fusion.300 = f32[1,1,128,512]{2,3,1,0:T(8,128)S(1)} fusion(f32[512,128]{1,0:T(8,128)S(1)} %fusion.299, s32[512]{0:T(512)S(1)} %iota_add_fusion.3, f32[1,128,2048]{2,1,0:T(8,128)S(1)} %copy-done.40), kind=kOutput, calls=%fused_computation.20.clone.1 | convolution fusion | flops 1625358336 | bytes 1574912 | tf_op jit(solution)/shard_map/while/body/eval_jaxpr/...n,nc->...c/dot_general | solution.py:72
  420.1 23.0 %fusion.301 = f32[512,128]{1,0:T(8,128)S(1)} fusion(s32[512]{0:T(512)S(1)} %iota_add_fusion.3, f32[1,128,2048]{2,1,0:T(8,128)} %get-tuple-element.221), kind=kOutput, calls=%fused_computation.14.clone.1 | convolution fusion | flops 1625292800 | bytes 1312768 | tf_op jit(solution)/shard_map/while/body/eval_jaxpr/...n,nc->...c/dot_general | solution.py:72
  443.1 22.2 %fusion.302 = f32[1,1,128,512]{2,3,1,0:T(8,128)S(1)} fusion(f32[512,128]{1,0:T(8,128)S(1)} %fusion.301, s32[512]{0:T(512)S(1)} %iota_add_fusion.3, f32[1,128,2048]{2,1,0:T(8,128)S(1)} %get-tuple-element.222), kind=kOutput, calls=%fused_computation.18.clone.1 | convolution fusion | flops 1625358336 | bytes 1574912 | tf_op jit(solution)/shard_map/while/body/eval_jaxpr/...n,nc->...c/dot_general | solution.py:72
  465.3 22.2 %fusion.299 = f32[512,128]{1,0:T(8,128)S(1)} fusion(s32[512]{0:T(512)S(1)} %iota_add_fusion.3, f32[1,128,2048]{2,1,0:T(8,128)S(1)} %get-tuple-element.222), kind=kOutput, calls=%fused_computation.13.clone.1 | convolution fusion | flops 1625292800 | bytes 1312768 | tf_op jit(solution)/shard_map/while/body/eval_jaxpr/...n,nc->...c/dot_general | solution.py:72
  487.6 22.1 %fusion.300 = f32[1,1,128,512]{2,3,1,0:T(8,128)S(1)} fusion(f32[512,128]{1,0:T(8,128)S(1)} %fusion.299, s32[512]{0:T(512)S(1)} %iota_add_fusion.3, f32[1,128,2048]{2,1,0:T(8,128)S(1)} %copy-done.40), kind=kOutput, calls=%fused_computation.20.clone.1 | convolution fusion | flops 1625358336 | bytes 1574912 | tf_op jit(solution)/shard_map/while/body/eval_jaxpr/...n,nc->...c/dot_general | solution.py:72
  520.7 23.5 %collective-permute-done = f32[2,1,128,1024]{2,3,0,1:T(8,128)S(1)} collective-permute-done((f32[2,1,128,1024]{2,3,0,1:T(8,128)S(1)}, f32[2,1,128,1024]{2,3,0,1:T(8,128)S(1)}, u32[]{:S(2)}, u32[]{:S(2)}) %collective-permute-start) | collective-permute-done | bytes 1048608 | tf_op jit(solution)/shard_map/ppermute | solution.py:29
  544.2 22.4 %collective-permute-done.1 = f32[2,1,128,1024]{2,3,0,1:T(8,128)} collective-permute-done((f32[2,1,128,1024]{2,3,0,1:T(8,128)S(1)}, f32[2,1,128,1024]{2,3,0,1:T(8,128)}, u32[]{:S(2)}, u32[]{:S(2)}) %collective-permute-start.1) | collective-permute-done | bytes 1048608 | tf_op jit(solution)/shard_map/ppermute | solution.py:29
  566.6 3.3 collective-permute-start.2
  572.3 18.3 %collective-permute-done.2 = f32[2,1,128,1024]{2,3,0,1:T(8,128)} collective-permute-done((f32[2,1,128,1024]{2,3,0,1:T(8,128)}, f32[2,1,128,1024]{2,3,0,1:T(8,128)}, u32[]{:S(2)}, u32[]{:S(2)}) %collective-permute-start.2) | collective-permute-done | bytes 1048608 | tf_op jit(solution)/shard_map/ppermute | solution.py:29
  593.4 3.8 slice.220
  602.3 4.9 all-to-all-start.1
  610.7 3.8 all-to-all-done.1
  614.6 3.4 all-to-all-start.2
  621.7 2.4 bitcast_select_fusion
  627.3 3.5 fusion.187
  630.8 4.6 collective-permute-start.3
  637.9 2.4 copy.103
  644.2 2.3 multiply_reduce_fusion.4
  648.8 3.3 fusion.189
  652.7 5.3 collective-permute-start.5
  661.1 2.3 copy.102
  663.4 2.3 copy.104
  671.8 2.3 multiply_reduce_fusion.3
  676.3 3.2 fusion.191
  680.1 5.5 collective-permute-start.7
  688.8 2.5 copy.105
  691.2 2.3 copy.107
  693.6 2.3 copy.109
  701.1 3.2 convolution_add_fusion
  704.3 2.9 copy.91
  707.2 2.9 fusion.184
  710.1 36.0 %psum.42 = f32[1,32,16]{2,1,0:T(8,128)} all-reduce(f32[1,32,16]{2,1,0:T(8,128)S(1)} %bitcast.395), channel_id=1, replica_groups=mesh['dp'=16,'freq'=8] {'freq'}, use_global_device_ids=true, to_apply=%region_5.6 | all-reduce | flops 512 | bytes 4096 | tf_op jit(solution)/shard_map/psum | solution.py:213
  753.4 3.3 multiply_convert_fusion.2
  756.8 3.6 fusion.190
  761.7 5.6 collective-permute-start.10
  769.1 2.5 copy.108
  771.6 2.4 fusion.91
  779.2 2.5 convolution_bitcast_fusion
  791.2 5.8 collective-permute-start.12
  811.3 5.5 collective-permute-start.14
  821.4 2.6 fusion.57
  826.2 79.6 %all-reduce = (f32[]{:T(128)}, f32[512,10]{0,1:T(8,128)}) all-reduce(f32[]{:T(128)S(6)} %mul.496, f32[512,10]{0,1:T(8,128)S(1)} %multiply_multiply_fusion), channel_id=1, replica_groups=mesh['dp'=16,'freq'=8] {'dp','freq'}, use_global_device_ids=true, to_apply=%region_8.9 | all-reduce | flops 5121 | bytes 40968 | tf_op jit(solution)/shard_map/psum | solution.py:268
  905.8 85.8 %all-reduce.4.cloned.1.call-done = (f32[256,512]{1,0:T(8,128)}, f32[3,3,16,512]{3,2,1,0:T(8,128)}, f32[3,512,512]{2,1,0:T(8,128)}) async-done(((f32[256,512]{1,0:T(8,128)}, f32[3,3,16,512]{3,2,1,0:T(8,128)}, f32[3,512,512]{2,1,0:T(8,128)}), (f32[256,512]{1,0:T(8,128)}, f32[3,3,16,512]{3,2,1,0:T(8,128)}, f32[3,512,512]{2,1,0:T(8,128)})) %all-reduce.4.cloned.1.call-update) | async-done | bytes 3964944 | tf_op jit(solution)/shard_map/psum | solution.py:268
  995.1 3.9 copy.171
  (290 shorter events, 108.3 us)
Async XLA Ops:
  7.2 618.7 %copy-start = (bf16[256,512]{1,0:T(8,128)(2,1)S(1)}, bf16[256,512]{1,0:T(8,128)(2,1)}, u32[]{:S(2)}) copy-start(bf16[256,512]{1,0:T(8,128)(2,1)} %param.10) | copy-start | bytes 786436
  7.2 20.3 %copy-start.67 = (f32[1,2,1024,256]{3,2,1,0:T(8,128)S(1)}, f32[1,2,1024,256]{3,2,1,0:T(8,128)}, u32[]{:S(2)}) copy-start(f32[1,2,1024,256]{3,2,1,0:T(8,128)} %param.9) | copy-start | bytes 6291460
  98.8 38.8 %all-to-all-start = ((f32[1,2,1024,256]{3,1,0,2:T(2,128)}), f32[1,2,1024,256]{3,1,0,2:T(2,128)S(1)}, u32[]{:S(2)}, u32[]{:S(2)}) async-start(f32[1,2,1024,256]{3,1,0,2:T(2,128)} %copy.83), calls=%async_computation | async-start | bytes 4194304 | tf_op jit(solution)/shard_map/all_to_all | solution.py:163
  189.7 22.2 %copy-start.40 = (f32[1,128,2048]{2,1,0:T(8,128)S(1)}, f32[1,128,2048]{2,1,0:T(8,128)}, u32[]{:S(2)}) copy-start(f32[1,128,2048]{2,1,0:T(8,128)} %get-tuple-element.221) | copy-start | bytes 3145732 | tf_op jit(solution)/shard_map/while
  281.7 22.0 %copy-start.40 = (f32[1,128,2048]{2,1,0:T(8,128)S(1)}, f32[1,128,2048]{2,1,0:T(8,128)}, u32[]{:S(2)}) copy-start(f32[1,128,2048]{2,1,0:T(8,128)} %get-tuple-element.221) | copy-start | bytes 3145732 | tf_op jit(solution)/shard_map/while
  373.5 22.0 %copy-start.40 = (f32[1,128,2048]{2,1,0:T(8,128)S(1)}, f32[1,128,2048]{2,1,0:T(8,128)}, u32[]{:S(2)}) copy-start(f32[1,128,2048]{2,1,0:T(8,128)} %get-tuple-element.221) | copy-start | bytes 3145732 | tf_op jit(solution)/shard_map/while
  465.3 22.2 %copy-start.40 = (f32[1,128,2048]{2,1,0:T(8,128)S(1)}, f32[1,128,2048]{2,1,0:T(8,128)}, u32[]{:S(2)}) copy-start(f32[1,128,2048]{2,1,0:T(8,128)} %get-tuple-element.221) | copy-start | bytes 3145732 | tf_op jit(solution)/shard_map/while
  518.1 51.8 %copy-start.66 = (s32[33]{0:T(128)S(1)}, s32[33]{0:T(128)}, u32[]{:S(2)}) copy-start(s32[33]{0:T(128)} %param.15) | copy-start | bytes 400
  519.4 24.7 %collective-permute-start = (f32[2,1,128,1024]{2,3,0,1:T(8,128)S(1)}, f32[2,1,128,1024]{2,3,0,1:T(8,128)S(1)}, u32[]{:S(2)}, u32[]{:S(2)}) collective-permute-start(f32[2,1,128,1024]{2,3,0,1:T(8,128)S(1)} %slice.266), channel_id=1, source_target_pairs={{0,1},{1,0},{2,3},{3,2},{4,5},{5,4},{6,7},{7,6},{8,9},{9,8},{10,11... | collective-permute-start | bytes 3145736 | tf_op jit(solution)/shard_map/ppermute | solution.py:29
  544.2 22.4 %collective-permute-start.1 = (f32[2,1,128,1024]{2,3,0,1:T(8,128)S(1)}, f32[2,1,128,1024]{2,3,0,1:T(8,128)}, u32[]{:S(2)}, u32[]{:S(2)}) collective-permute-start(f32[2,1,128,1024]{2,3,0,1:T(8,128)S(1)} %collective-permute-done), channel_id=1, source_target_pairs={{0,2},{1,3},{2,0},{3,1},{4,6},{5,7},{6,4},{7,5},{8,10},{9,11},{10,... | collective-permute-start | bytes 3145736 | tf_op jit(solution)/shard_map/ppermute | solution.py:29
  566.6 24.0 %collective-permute-start.2 = (f32[2,1,128,1024]{2,3,0,1:T(8,128)}, f32[2,1,128,1024]{2,3,0,1:T(8,128)}, u32[]{:S(2)}, u32[]{:S(2)}) collective-permute-start(f32[2,1,128,1024]{2,3,0,1:T(8,128)} %collective-permute-done.1), channel_id=1, source_target_pairs={{0,4},{1,5},{2,6},{3,7},{4,0},{5,1},{6,2},{7,3},{8,12},{9,13},{10,... | collective-permute-start | bytes 3145736 | tf_op jit(solution)/shard_map/ppermute | solution.py:29
  569.9 22.7 %copy-start.60 = (pred[512]{0:T(512)(128)(4,1)}, pred[512]{0:T(512)(128)(4,1)S(1)}, u32[]{:S(2)}) copy-start(pred[512]{0:T(512)(128)(4,1)S(1)} %fusion.207) | copy-start | bytes 1540
  570.0 51.7 %copy-start.58 = (s32[32,16]{0,1:T(8,128)}, s32[32,16]{0,1:T(8,128)S(1)}, u32[]{:S(2)}) copy-start(s32[32,16]{0,1:T(8,128)S(1)} %broadcast_add_fusion) | copy-start | bytes 6148
  572.3 24.9 %copy-start.30 = (f32[4,2,1,128,512]{3,4,0,1,2:T(8,128)S(1)}, f32[4,2,1,128,512]{3,4,0,1,2:T(8,128)}, u32[]{:S(2)}) copy-start(f32[4,2,1,128,512]{3,4,0,1,2:T(8,128)} %get-tuple-element.83) | copy-start | bytes 6291460
  598.4 8.9 copy-start.41
  598.4 8.9 copy-start.31
  601.6 17.1 %copy-start.44 = (f32[512,10]{0,1:T(8,128)S(1)}, f32[512,10]{0,1:T(8,128)}, u32[]{:S(2)}) copy-start(f32[512,10]{0,1:T(8,128)} %param.13) | copy-start | bytes 61444
  602.3 12.2 %all-to-all-start.1 = ((bf16[8,2,8192]{2,1,0:T(2,128)(2,1)}), bf16[8,2,8192]{2,1,0:T(2,128)(2,1)S(1)}, u32[]{:S(2)}, u32[]{:S(2)}) async-start(bf16[8,2,8192]{2,1,0:T(2,128)(2,1)} %reshape.996), calls=%async_computation.1 | async-start | bytes 524288 | tf_op jit(solution)/shard_map/all_to_all | solution.py:178
  607.3 14.3 %copy-start.59 = (s32[32,16]{0,1:T(8,128)}, s32[32,16]{0,1:T(8,128)S(1)}, u32[]{:S(2)}) copy-start(s32[32,16]{0,1:T(8,128)S(1)} %fusion.203) | copy-start | bytes 6148
  614.6 10.6 %all-to-all-start.2 = ((bf16[8,2,8192]{2,1,0:T(2,128)(2,1)}), bf16[8,2,8192]{2,1,0:T(2,128)(2,1)S(1)}, u32[]{:S(2)}, u32[]{:S(2)}) async-start(bf16[8,2,8192]{2,1,0:T(2,128)(2,1)} %reshape.994), calls=%async_computation.2 | async-start | bytes 524288 | tf_op jit(solution)/shard_map/all_to_all | solution.py:179
  618.0 373.5 %all-reduce.4.cloned.1.call-start = ((), (), s32[]{:S(2)}) async-start(), calls=%async_computation.3 | async-start | bytes 7929856 | tf_op jit(solution)/shard_map/psum | solution.py:268
  621.6 2.4 slice-start
  621.6 2.4 slice-start.1
  621.7 2.4 copy-start.61
  627.0 8.3 copy-start.47
  627.2 15.1 %copy-start.9 = (bf16[1,1024,512]{2,1,0:T(8,128)(2,1)}, bf16[1,1024,512]{2,1,0:T(8,128)(2,1)S(1)}, u32[]{:S(2)}) copy-start(bf16[1,1024,512]{2,1,0:T(8,128)(2,1)S(1)} %fusion.277) | copy-start | bytes 3145732
  630.8 9.5 collective-permute-start.3
  636.6 5.8 collective-permute-start.4
  640.3 2.1 copy-start.18
  644.2 2.3 copy-start.25
  646.5 2.3 copy-start.1
  647.4 22.4 %copy-start.7 = (bf16[1,1024,512]{2,1,0:T(8,128)(2,1)}, bf16[1,1024,512]{2,1,0:T(8,128)(2,1)S(1)}, u32[]{:S(2)}) copy-start(bf16[1,1024,512]{2,1,0:T(8,128)(2,1)S(1)} %fusion.276) | copy-start | bytes 3145732
  648.8 10.5 %copy-start.10 = (bf16[1,1024,512]{2,1,0:T(8,128)(2,1)S(1)}, bf16[1,1024,512]{2,1,0:T(8,128)(2,1)}, u32[]{:S(2)}) copy-start(bf16[1,1024,512]{2,1,0:T(8,128)(2,1)} %copy-done.9) | copy-start | bytes 3145732
  652.7 15.2 %collective-permute-start.5 = (bf16[1,1,512]{2,1,0:T(2,128)(2,1)}, bf16[1,1,512]{2,1,0:T(2,128)(2,1)S(1)}, u32[]{:S(2)}, u32[]{:S(2)}) collective-permute-start(bf16[1,1,512]{2,1,0:T(2,128)(2,1)} %get-tuple-element.134), channel_id=1, source_target_pairs={{0,1},{1,2},{2,3},{3,4},{4,5},{5,6},{6,7},{8,9},{9,10},{10,11},{11... | collective-permute-start | bytes 3080 | tf_op jit(solution)/shard_map/ppermute | solution.py:22
  658.0 11.8 %collective-permute-start.6 = (bf16[1,1,512]{2,1,0:T(2,128)(2,1)}, bf16[1,1,512]{2,1,0:T(2,128)(2,1)S(1)}, u32[]{:S(2)}, u32[]{:S(2)}) collective-permute-start(bf16[1,1,512]{2,1,0:T(2,128)(2,1)} %get-tuple-element.133), channel_id=1, source_target_pairs={{1,0},{2,1},{3,2},{4,3},{5,4},{6,5},{7,6},{9,8},{10,9},{11,10},{12... | collective-permute-start | bytes 3080 | tf_op jit(solution)/shard_map/ppermute | solution.py:23
  669.8 2.0 copy-start.2
  671.8 2.3 copy-start.27
  674.1 2.1 copy-start.4
  676.3 10.6 %copy-start.8 = (bf16[1,1024,512]{2,1,0:T(8,128)(2,1)S(1)}, bf16[1,1024,512]{2,1,0:T(8,128)(2,1)}, u32[]{:S(2)}) copy-start(bf16[1,1024,512]{2,1,0:T(8,128)(2,1)} %copy-done.7) | copy-start | bytes 3145732
  680.1 15.8 %collective-permute-start.7 = (bf16[1,1,512]{2,1,0:T(2,128)(2,1)}, bf16[1,1,512]{2,1,0:T(2,128)(2,1)S(1)}, u32[]{:S(2)}, u32[]{:S(2)}) collective-permute-start(bf16[1,1,512]{2,1,0:T(2,128)(2,1)} %get-tuple-element.132), channel_id=1, source_target_pairs={{0,1},{1,2},{2,3},{3,4},{4,5},{5,6},{6,7},{8,9},{9,10},{10,11},{11... | collective-permute-start | bytes 3080 | tf_op jit(solution)/shard_map/ppermute | solution.py:22
  685.6 12.2 %collective-permute-start.8 = (bf16[1,1,512]{2,1,0:T(2,128)(2,1)}, bf16[1,1,512]{2,1,0:T(2,128)(2,1)S(1)}, u32[]{:S(2)}, u32[]{:S(2)}) collective-permute-start(bf16[1,1,512]{2,1,0:T(2,128)(2,1)} %get-tuple-element.131), channel_id=1, source_target_pairs={{1,0},{2,1},{3,2},{4,3},{5,4},{6,5},{7,6},{9,8},{10,9},{11,10},{12... | collective-permute-start | bytes 3080 | tf_op jit(solution)/shard_map/ppermute | solution.py:23
  695.9 3.9 copy-start.64
  697.8 3.3 copy-start.5
  746.9 2.9 copy-start.42
  756.8 3.6 copy-start.19
  756.8 10.5 %copy-start.56 = (bf16[1,1,512]{2,1,0:T(2,128)(2,1)S(1)}, bf16[1,1,512]{2,1,0:T(2,128)(2,1)}, u32[]{:S(2)}) copy-start(bf16[1,1,512]{2,1,0:T(2,128)(2,1)} %copy-done.55) | copy-start | bytes 3076
  756.8 10.5 %copy-start.65 = (bf16[1,1,512]{2,1,0:T(2,128)(2,1)S(1)}, bf16[1,1,512]{2,1,0:T(2,128)(2,1)}, u32[]{:S(2)}) copy-start(bf16[1,1,512]{2,1,0:T(2,128)(2,1)} %copy-done.64) | copy-start | bytes 3076
  760.4 21.4 %collective-permute-start.9 = (bf16[1,1,512]{2,1,0:T(2,128)(2,1)S(1)}, bf16[1,1,512]{2,1,0:T(2,128)(2,1)S(1)}, u32[]{:S(2)}, u32[]{:S(2)}) collective-permute-start(bf16[1,1,512]{2,1,0:T(2,128)(2,1)S(1)} %get-tuple-element.130), channel_id=1, source_target_pairs={{1,0},{2,1},{3,2},{4,3},{5,4},{6,5},{7,6},{9,8},{10,9},{11,10},{12... | collective-permute-start | bytes 3080 | tf_op jit(solution)/shard_map/ppermute | solution.py:23
  761.7 9.9 copy-start.51
  761.7 20.8 %collective-permute-start.10 = (bf16[1,1,512]{2,1,0:T(2,128)(2,1)S(1)}, bf16[1,1,512]{2,1,0:T(2,128)(2,1)S(1)}, u32[]{:S(2)}, u32[]{:S(2)}) collective-permute-start(bf16[1,1,512]{2,1,0:T(2,128)(2,1)S(1)} %get-tuple-element.129), channel_id=1, source_target_pairs={{0,1},{1,2},{2,3},{3,4},{4,5},{5,6},{6,7},{8,9},{9,10},{10,11},{11... | collective-permute-start | bytes 3080 | tf_op jit(solution)/shard_map/ppermute | solution.py:22
  771.6 2.4 copy-start.20
  771.6 2.4 copy-start.39
  777.0 2.1 copy-start.15
  777.0 2.1 copy-start.57
  779.1 2.6 copy-start.13
  779.1 3.4 copy-start.14
  784.4 2.0 copy-start.68
  789.0 8.0 copy-start.38
  789.8 8.0 copy-start.36
  789.8 9.9 collective-permute-start.11
  791.2 9.3 collective-permute-start.12
  810.0 9.5 collective-permute-start.13
  811.3 9.0 collective-permute-start.14
  824.0 2.1 copy-start.63
  (29 other events, 41.9 us)
Sparse Core Ops, SparseCore 0:
  824.1 167.3 all-reduce.3
where the time goes:
time: 1020 us; the launch traced here: 1010 us
  matrix products  513 us (50%)
  waiting for transfers between devices  185 us (18%)
  blocking collectives  116 us (11%)
  local copies, waits for them, and re-layouts  68.2 us (7%)
  starting transfers between devices  61.3 us (6%)
  other arithmetic  34.4 us (3%)
  between operations  17.9 us (2%)
  loops' own time  11.4 us (1%)
    dot_general x16, matrix products, table_product(): return jnp.einsum('...n,nc->...c', values, table, precision=EXACT_DOTS)  358 us
    dot_general x4, matrix products, table_product(): return jnp.einsum('kn,...nm->...km', table, values, precision=EXACT_DOTS)  88.4 us
    psum x1, waiting for transfers between devices, local(): lax.psum((loss_part, grad_stem, jnp.stack(conv_grads), jnp.stack(mix_grad...  85.8 us
    psum x1, blocking collectives, local(): lax.psum((loss_part, grad_stem, jnp.stack(conv_grads), jnp.stack(mix_grad...  79.6 us
    ppermute x3, waiting for transfers between devices, from_partner(): lax.ppermute(x, axis, [(i, i ^ 1 << stride) for i in range(lax.axis_size(...  64.2 us
    psum x1, blocking collectives, local(): band_sum = lax.psum(partial_value, 'freq')  36 us
    ppermute x6, starting transfers between devices, with_halo(): before = lax.ppermute(last, axis, up)  32.3 us
    all_to_all x1, waiting for transfers between devices, local(): lax.all_to_all(stacked, 'freq', split_axis=2, concat_axis=3, tiled=True)  30.6 us
  transfers between devices with their start and end apart: 19, of which 8 were waited for; matrix products, arithmetic and copies ran while one was open for 6% of the time, Pallas kernels for 0%

commit v1 on v0

v1 whole, which is shorter than its diff:
```python
import functools

import jax
import jax.numpy as jnp
import numpy as np
from jax import lax
from jax.experimental import pallas as pl
from jax.experimental.pallas import tpu as pltpu
from jax.sharding import PartitionSpec as P

EXACT_DOTS = lax.Precision.HIGHEST
EPS = 1e-05
N1 = 1024
N2 = 2048
TOTAL = N1 * N2
POOL = 128
GROUP_WIDTH = 16
KW = 3
PARTS = 8
COLS = N2 // PARTS
HALO = 8
BLOCK_ROWS = N2 // 2 // PARTS + 2 * HALO
BF16 = jnp.bfloat16
F32 = jnp.float32


def split_host(values):
    high = np.asarray(values, np.float32).astype(jnp.bfloat16)
    low = (values - high.astype(np.float64)).astype(jnp.bfloat16)
    return high, low


def first_tables():
    rows = np.arange(N1 // 2, dtype=np.int64)[:, None]
    samples = np.arange(N1 // 2, dtype=np.int64)[None]
    angles = -np.pi * (samples * (2 * rows + 1) % (2 * N1)) / N1
    blocks = [np.cos(angles).reshape(4, 128, -1), np.sin(angles).reshape(4, 128, -1)]
    return split_host(np.stack(blocks, axis=1).reshape(4 * 256, N1 // 2))


def turn_tables():
    rows = np.arange(N1 // 2, dtype=np.int64)[:, None]
    columns = np.arange(COLS, dtype=np.int64)[None]
    angles = -np.pi * (columns * (2 * rows + 1)) / TOTAL
    device_angles = -np.pi * (COLS * np.arange(PARTS, dtype=np.int64)[None] * (2 * rows + 1)) / TOTAL
    shared = np.stack([np.cos(angles), np.sin(angles)]).astype(np.float32)
    own = np.concatenate([np.cos(device_angles), np.sin(device_angles)], axis=1).astype(np.float32)
    return shared, own


def second_tables():
    order = np.concatenate([np.arange(128), np.arange(255, 127, -1)]).astype(np.int64)
    columns = np.arange(COLS, dtype=np.int64)[None]
    angles = -2 * np.pi * (order[:, None] * columns % COLS) / COLS
    cosine, sine = np.cos(angles), np.sin(angles)
    upper = np.concatenate([cosine, -sine], axis=1)
    lower = np.concatenate([sine, cosine], axis=1)
    lanes = -2 * np.pi * (np.arange(PARTS, dtype=np.int64)[:, None] * columns) / N2
    turn = np.concatenate([np.cos(lanes), np.sin(lanes)], axis=0).astype(np.float32)
    return split_host(np.concatenate([upper, lower], axis=0)) + (turn,)


def three_pass(lhs_high, lhs_low, rhs_high, rhs_low, dims):
    product = functools.partial(
        lax.dot_general, dimension_numbers=(dims, ((), ())), preferred_element_type=F32
    )
    return product(lhs_high, rhs_high) + (product(lhs_high, rhs_low) + product(lhs_low, rhs_high))


def first_kernel(x_ref, th_ref, tl_ref, turn_ref, own_ref, out_ref, xh_ref, xl_ref):
    @pl.when(pl.program_id(0) == 0)
    def _():
        for channel in range(2):
            for piece in range(4):
                rows = pl.ds(piece * 256, 256)
                value = x_ref[channel, rows, :]
                high = value.astype(BF16)
                xh_ref[channel, rows, :] = high
                xl_ref[channel, rows, :] = (value - high.astype(F32)).astype(BF16)

    place = lax.axis_index("freq")
    lane = lax.broadcasted_iota(jnp.int32, (128, 2 * PARTS), 1)
    own = own_ref[...]
    own_cos = jnp.sum(jnp.where(lane == place, own, 0.0), axis=1, keepdims=True)
    own_sin = jnp.sum(jnp.where(lane == place + PARTS, own, 0.0), axis=1, keepdims=True)
    cosine = turn_ref[0] * own_cos - turn_ref[1] * own_sin
    sine = turn_ref[0] * own_sin + turn_ref[1] * own_cos
    row = lax.broadcasted_iota(jnp.int32, (128, COLS), 0)
    sign = jnp.where(row % 2 == 0, 1.0, -1.0)
    for channel in range(2):
        parts = []
        for half in range(2):
            rows = pl.ds(half * 512, 512)
            parts.append(
                three_pass(
                    th_ref[...], tl_ref[...], xh_ref[channel, rows, :], xl_ref[channel, rows, :],
                    ((1,), (0,)),
                )
            )
        real = parts[0][:128] + sign * parts[1][128:]
        imag = parts[0][128:] - sign * parts[1][:128]
        out_ref[channel, 0] = (real * cosine - imag * sine).astype(BF16)
        out_ref[channel, 1] = (real * sine + imag * cosine).astype(BF16)


def first_section(records):
    table_high, table_low = first_tables()
    shared, own = turn_tables()
    return pl.pallas_call(
        first_kernel,
        grid=(4,),
        out_shape=jax.ShapeDtypeStruct((PARTS, 2, 128, COLS), BF16),
        in_specs=[
            pl.BlockSpec((2, N1, COLS), lambda j: (0, 0, 0)),
            pl.BlockSpec((256, 512), lambda j: (j, 0)),
            pl.BlockSpec((256, 512), lambda j: (j, 0)),
            pl.BlockSpec((2, 128, COLS), lambda j: (0, j, 0)),
            pl.BlockSpec((128, 2 * PARTS), lambda j: (j, 0)),
        ],
        out_specs=pl.BlockSpec((2, 2, 128, COLS), lambda j: (j, 0, 0, 0)),
        scratch_shapes=[pltpu.VMEM((2, N1, COLS), BF16)] * 2,
        name="first_section",
    )(records, jnp.asarray(table_high), jnp.asarray(table_low), jnp.asarray(shared), jnp.asarray(own))


def eight_point(values):
    root = np.float32(np.sqrt(0.5))

    def add(a, b):
        return (a[0] + b[0], a[1] + b[1])

    def sub(a, b):
        return (a[0] - b[0], a[1] - b[1])

    def quarter(a):
        return (a[1], -a[0])

    def four(a):
        s02, d02, s13, d13 = add(a[0], a[2]), sub(a[0], a[2]), add(a[1], a[3]), sub(a[1], a[3])
        turned = quarter(d13)
        return [add(s02, s13), add(d02, turned), sub(s02, s13), sub(d02, turned)]

    even, odd = four(values[0::2]), four(values[1::2])
    turned = [
        odd[0],
        ((odd[1][0] + odd[1][1]) * root, (odd[1][1] - odd[1][0]) * root),
        quarter(odd[2]),
        ((odd[3][1] - odd[3][0]) * root, -(odd[3][0] + odd[3][1]) * root),
    ]
    return [add(even[i], turned[i]) for i in range(4)] + [sub(even[i], turned[i]) for i in range(4)]


def combine_columns(load, turn_ref, wh_ref, wl_ref):
    rows_at_once = 16

    def step(index, carry):
        rows = pl.ds(pl.multiple_of(index * rows_at_once, rows_at_once), rows_at_once)
        values = [
            (load(part, 0, rows).astype(F32), load(part, 1, rows).astype(F32))
            for part in range(PARTS)
        ]
        for u, (real, imag) in enumerate(eight_point(values)):
            if u:
                cosine, sine = turn_ref[u : u + 1, :], turn_ref[PARTS + u : PARTS + u + 1, :]
                real, imag = real * cosine - imag * sine, real * sine + imag * cosine
            for side, value in enumerate((real, imag)):
                high = value.astype(BF16)
                wh_ref[u, rows, side * COLS : (side + 1) * COLS] = high
                wl_ref[u, rows, side * COLS : (side + 1) * COLS] = (value - high.astype(F32)).astype(BF16)
        return carry

    lax.fori_loop(0, 128 // rows_at_once, step, 0)


def bins_to_features(dh_ref, dl_ref, wh_ref, wl_ref, feat_ref):
    lower_rows = N2 // 2
    for side in range(2):
        feat_ref[side, 0:HALO, :] = jnp.zeros((HALO, 128), F32)
        feat_ref[side, HALO + lower_rows :, :] = jnp.zeros((HALO, 128), F32)
    for pair in range(4):
        wh = wh_ref[2 * pair : 2 * pair + 2].reshape(256, 2 * COLS)
        wl = wl_ref[2 * pair : 2 * pair + 2].reshape(256, 2 * COLS)
        out = three_pass(dh_ref[...], dl_ref[...], wh, wl, ((1,), (1,)))
        power = out[:256] * out[:256] + out[256:] * out[256:]
        feature = jnp.log1p(power * np.float32(1.0 / TOTAL))
        for k in range(2):
            u = 2 * pair + k
            lanes = slice(128 * k, 128 * k + 128)
            feat_ref[0, pl.ds(HALO + u, 128, stride=8), :] = feature[:128, lanes]
            feat_ref[1, pl.ds(HALO + 7 - u, 128, stride=8), :] = feature[128:, lanes]


def second_kernel(x_ref, dh_ref, dl_ref, turn_ref, out_ref, wh_ref, wl_ref, feat_ref):
    combine_columns(lambda part, side, rows: x_ref[part, side, rows, :], turn_ref, wh_ref, wl_ref)
    bins_to_features(dh_ref, dl_ref, wh_ref, wl_ref, feat_ref)
    row = lax.broadcasted_iota(jnp.int32, (128, 128), 0)
    col = lax.broadcasted_iota(jnp.int32, (128, 128), 1)
    mirror = jnp.where(row + col == 127, 1.0, 0.0).astype(BF16)
    for target in range(PARTS):
        rows = pl.ds(target * 128, BLOCK_ROWS)
        out_ref[target, 0] = feat_ref[0, rows, :].astype(BF16)
        out_ref[target, 1] = jnp.dot(
            feat_ref[1, rows, :].astype(BF16), mirror, preferred_element_type=F32
        ).astype(BF16)


def second_section(exchanged):
    table_high, table_low, turn = second_tables()
    return pl.pallas_call(
        second_kernel,
        out_shape=jax.ShapeDtypeStruct((PARTS, 2, BLOCK_ROWS, 128), BF16),
        scratch_shapes=[
            pltpu.VMEM((PARTS, 128, 2 * COLS), BF16),
            pltpu.VMEM((PARTS, 128, 2 * COLS), BF16),
            pltpu.VMEM((2, N2 // 2 + 2 * HALO, 128), F32),
        ],
        name="second_section",
    )(exchanged, jnp.asarray(table_high), jnp.asarray(table_low), jnp.asarray(turn))


def group_mask(channels):
    row_group = lax.broadcasted_iota(jnp.int32, (channels, channels), 0) // GROUP_WIDTH
    col_group = lax.broadcasted_iota(jnp.int32, (channels, channels), 1) // GROUP_WIDTH
    return row_group == col_group


def dense_taps(tap_weights):
    channels = tap_weights.shape[-1]
    tiled = jnp.tile(tap_weights, (1, channels // GROUP_WIDTH, 1))
    return jnp.where(group_mask(channels)[None], tiled, jnp.zeros_like(tiled))


def matmul(a, b, dims):
    return lax.dot_general(a, b, (dims, ((), ())), preferred_element_type=F32)


def local(records, stem_weight, conv_weight, mix_weight, head_weight, labels, band_bounds):
    place = lax.axis_index("freq")
    exchanged = lax.all_to_all(first_section(records[0]), "freq", 0, 0, tiled=True)
    blocks = lax.all_to_all(second_section(exchanged), "freq", 0, 0, tiled=True)
    own_len = TOTAL // 2 // POOL // PARTS
    length = own_len + 16
    blocks = blocks.reshape(4, 2, 2, BLOCK_ROWS, 128)[:, :, :, HALO - 1 : HALO + 129]
    ordered = jnp.concatenate([blocks[:, :, 0], blocks[::-1, :, 1]], axis=0)
    positions = ordered.transpose(2, 0, 1, 3).reshape(length, 256)
    own = slice(8, 8 + own_len)
    q = place * own_len - 8 + lax.broadcasted_iota(jnp.int32, (length, 1), 0)
    valid = (q >= 0) & (q < own_len * PARTS)
    channels = stem_weight.shape[1]
    groups = channels // GROUP_WIDTH
    layers = conv_weight.shape[0]
    stream = matmul(positions, stem_weight, ((1,), (0,)))
    saved = []
    for layer in range(layers):
        dense = dense_taps(conv_weight[layer])
        scale = lax.rsqrt(jnp.mean(stream * stream, axis=-1, keepdims=True) + EPS)
        normed = jnp.where(valid, stream * scale, 0.0).astype(BF16)
        padded = jnp.pad(normed, ((1, 1), (0, 0)))
        preact = sum(matmul(padded[t : t + length], dense[t], ((1,), (0,))) for t in range(KW))
        activated = jax.nn.silu(preact).astype(BF16)
        saved.append((stream, scale, padded, preact, activated, dense))
        stream = stream + matmul(activated, mix_weight[layer], ((1,), (0,)))
    low = jnp.repeat(band_bounds[:-1], GROUP_WIDTH)[None]
    high = jnp.repeat(band_bounds[1:], GROUP_WIDTH)[None]
    counts = ((high - low) // POOL).astype(F32)
    member = (q * POOL >= low) & (q * POOL < high)
    partial_sum = jnp.sum(jnp.where(member, stream, 0.0)[own], axis=0, keepdims=True)
    gathered = lax.all_to_all(
        jnp.broadcast_to(partial_sum[None], (PARTS, 8, channels)), "freq", 0, 0, tiled=True
    )
    pooled = jnp.sum(gathered, axis=0)[:1] / counts
    logits = jnp.dot(pooled, head_weight, precision=EXACT_DOTS)
    exponents = jnp.exp(logits)
    denominator = jnp.sum(exponents, axis=-1, keepdims=True)
    classes = head_weight.shape[1]
    one_hot = (labels[:, None] == lax.broadcasted_iota(jnp.int32, (1, classes), 1)).astype(F32)
    all_records = lax.axis_size("dp")
    lead = (place == 0).astype(F32)
    loss = (jnp.log(denominator[0, 0]) - jnp.sum(one_hot * logits)) / all_records * lead
    grad_logits = (exponents / denominator - one_hot) / all_records
    head_part = grad_logits.T * pooled * lead
    grad_band = jnp.dot(grad_logits, head_weight.T, precision=EXACT_DOTS) / counts
    grad_stream = jnp.where(member, grad_band, 0.0)
    conv_grads, mix_grads = [None] * layers, [None] * layers
    group_row = lax.broadcasted_iota(jnp.int32, (groups, GROUP_WIDTH, channels), 0)
    group_col = lax.broadcasted_iota(jnp.int32, (groups, GROUP_WIDTH, channels), 2) // GROUP_WIDTH
    for layer in reversed(range(layers)):
        stream_in, scale, padded, preact, activated, dense = saved[layer]
        grad_out = grad_stream.astype(BF16)
        mix_grads[layer] = matmul(activated[own], grad_out[own], ((0,), (0,)))
        grad_act = matmul(grad_out, mix_weight[layer], ((1,), (1,)))
        gate = jax.nn.sigmoid(preact)
        grad_pre = grad_act * gate * (1.0 + preact * (1.0 - gate))
        grad_pre = jnp.where(valid, grad_pre, 0.0).astype(BF16)
        own_pre = grad_pre[own]
        taps = []
        for t in range(KW):
            full = matmul(padded[8 + t : 8 + t + own_len], own_pre, ((0,), (0,)))
            full = full.reshape(groups, GROUP_WIDTH, channels)
            taps.append(jnp.sum(jnp.where(group_row == group_col, full, 0.0), axis=0))
        conv_grads[layer] = jnp.concatenate(taps, axis=0)
        grad_padded = jnp.pad(grad_pre, ((1, 1), (0, 0)))
        grad_normed = sum(
            matmul(grad_padded[2 - t : 2 - t + length], dense[t], ((1,), (1,))) for t in range(KW)
        )
        grad_stream = (
            grad_stream
            + scale * grad_normed
            - stream_in * scale**3 * jnp.mean(stream_in * grad_normed, axis=-1, keepdims=True)
        )
    rounded = lax.reduce_precision(grad_stream, 8, 7)
    grad_high = rounded.astype(BF16)
    grad_low = (grad_stream - rounded).astype(BF16)
    own_positions = positions[own]
    grad_stem = matmul(own_positions, grad_high[own], ((0,), (0,))) + matmul(
        own_positions, grad_low[own], ((0,), (0,))
    )
    pieces = [grad_stem] + conv_grads + mix_grads + [
        jnp.pad(head_part, ((0, 16 - classes), (0, 0))).at[15, 0].set(loss)
    ]
    packed = lax.psum(jnp.concatenate(pieces, axis=0), ("dp", "freq"))
    stem_rows = positions.shape[1]
    conv_rows = stem_rows + layers * KW * GROUP_WIDTH
    mix_rows = conv_rows + layers * channels
    return (
        packed[mix_rows + 15, 0],
        packed[:stem_rows],
        packed[stem_rows:conv_rows].reshape(layers, KW, GROUP_WIDTH, channels),
        packed[conv_rows:mix_rows].reshape(layers, channels, channels),
        packed[mix_rows : mix_rows + classes].T,
    )


def solution(mesh):
    in_specs = (P("dp", None, None, "freq"), P(), P(), P(), P(), P("dp"), P())
    out_specs = (P(), P(), P(), P(), P())
    return jax.shard_map(local, mesh=mesh, in_specs=in_specs, out_specs=out_specs, check_vma=False)
```

time: 1020 us -> 333 us (0.33); the launches traced: 1010 us -> 332 us
  matrix products: 513 us -> 55.4 us
  blocking collectives: 116 us -> 0 us
  starting transfers between devices: 61.3 us -> 16.7 us
  local copies, waits for them, and re-layouts: 68.2 us -> 35.9 us
  other arithmetic: 34.4 us -> 17.1 us
  Pallas kernels: 0 us -> 12.9 us
  loops' own time: 11.4 us -> 0 us
    dot_general x59 -> x40, matrix products: 511 us -> 54.7 us  [the longest x39 54.5 us: matmul(): return lax.dot_general(a, b, (dims, ((), ())), preferred_element_type=F32)]
    psum x2 -> x0, blocking collectives: 116 us -> none  [the longest x1 79.6 us: local(): lax.psum((loss_part, grad_stem, jnp.stack(conv_grads), jnp.stack(mix_grad...]
    psum x1, waiting for transfers between devices: 85.8 us -> 154 us  [local(): packed = lax.psum(jnp.concatenate(pieces, axis=0), ('dp', 'freq'))]
    ppermute x15 -> x0, waiting for transfers between devices: 64.4 us -> none  [the longest x3 64.2 us: from_partner(): lax.ppermute(x, axis, [(i, i ^ 1 << stride) for i in range(lax.axis_size(...]
    ppermute x15 -> x0, starting transfers between devices: 44.8 us -> none  [the longest x6 32.3 us: with_halo(): before = lax.ppermute(last, axis, up)]
    dot_general x7 -> x0, local copies, waits for them, and re-layouts: 15 us -> none  [the longest x6 14.2 us: conv_weight_grad(): jnp.einsum('rpc,rpd->cd', window, grad_pre, preferred_element_type=jnp.fl...]
    pallas_call x0 -> x2, Pallas kernels: none -> 12.9 us  [the longest x1 7.32 us: first_section(): pl.pallas_call(first_kernel, grid=(4,), out_shape=jax.ShapeDtypeStruct((P...]
    another operation x1 -> x0, loops' own time: 11.4 us -> none  [second_section(): blocks = lax.map(one_block, jnp.arange(columns // block_width))]
  transfers between devices with their start and end apart: 19 -> 4, of which waited for: 8 -> 4; matrix products, arithmetic and copies ran while one was open for 6% -> 3% of each run, Pallas kernels for 0% -> 0%
where the time goes in v1:
time: 333 us; the launch traced here: 332 us
  waiting for transfers between devices  177 us (53%)
  matrix products  55.4 us (17%)
  local copies, waits for them, and re-layouts  35.9 us (11%)
  other arithmetic  17.1 us (5%)
  starting transfers between devices  16.7 us (5%)
  between operations  16.6 us (5%)
  Pallas kernels  12.9 us (4%)
    psum x1, waiting for transfers between devices, local(): packed = lax.psum(jnp.concatenate(pieces, axis=0), ('dp', 'freq'))  154 us
    dot_general x39, matrix products, matmul(): return lax.dot_general(a, b, (dims, ((), ())), preferred_element_type=F32)  54.5 us
    unnamed x111, local copies, waits for them, and re-layouts  18.4 us
    all_to_all x1, waiting for transfers between devices, local(): lax.all_to_all(first_section(records[0]), 'freq', 0, 0, tiled=True)  13.9 us
    all_to_all x1, starting transfers between devices, local(): lax.all_to_all(first_section(records[0]), 'freq', 0, 0, tiled=True)  8.28 us
    pallas_call x1, Pallas kernels, first_section(): pl.pallas_call(first_kernel, grid=(4,), out_shape=jax.ShapeDtypeStruct((P...  7.32 us
  transfers between devices with their start and end apart: 4, of which 4 were waited for; matrix products, arithmetic and copies ran while one was open for 3% of the time, Pallas kernels for 0%

profile of v1, /device:TPU:1, one launch (start us, length us, event | category | flops | bytes accessed | tf_op | source)
XLA Modules:
  0.0 331.8 jit_solution(18363327589668164111)
XLA Ops:
  7.2 7.3 %first_section.1 = bf16[8,2,128,256]{3,2,1,0:T(8,128)(2,1)} custom-call(f32[2,1024,256]{2,1,0:T(8,128)} %bitcast.146, bf16[1024,512]{1,0:T(8,128)(2,1)} %constant.151.clone.th_ref, bf16[1024,512]{1,0:T(8,128)(2,1)} %constant.152.clone.tl_ref, f32[2,512,256]{2,1,0:T(8,128)} %constant.153.clone.turn_ref, f32[512,16]{1,0:T(8,128)} %constant.154.clone.own_ref), custom_call_target="tpu_custom_call" | custom-call | tf_op jit(solution)/shard_map/first_section/pallas_call | solution.py:109
  14.5 8.3 %all-to-all-start = ((bf16[8,2,128,256]{3,2,1,0:T(8,128)(2,1)}), bf16[8,2,128,256]{3,2,1,0:T(8,128)(2,1)S(1)}, u32[]{:S(2)}, u32[]{:S(2)}) async-start(bf16[8,2,128,256]{3,2,1,0:T(8,128)(2,1)} %first_section.1), calls=%async_computation | async-start | bytes 2097152 | tf_op jit(solution)/shard_map/all_to_all | solution.py:239
  23.6 1.0 select_compare_fusion.1
  24.5 13.9 %all-to-all-done.x_ref = bf16[8,2,128,256]{3,2,1,0:T(8,128)(2,1)S(1)} async-done(((bf16[8,2,128,256]{3,2,1,0:T(8,128)(2,1)}), bf16[8,2,128,256]{3,2,1,0:T(8,128)(2,1)S(1)}, u32[]{:S(2)}, u32[]{:S(2)}) %all-to-all-start) | async-done | bytes 1048608 | tf_op jit(solution)/shard_map/all_to_all | solution.py:239
  38.4 1.0 copy-done.20
  39.4 5.6 %second_section.1 = bf16[8,2,144,128]{3,2,1,0:T(8,128)(2,1)} custom-call(bf16[8,2,128,256]{3,2,1,0:T(8,128)(2,1)} %copy-done.20, bf16[512,512]{1,0:T(8,128)(2,1)} %constant.155.clone.dh_ref, bf16[512,512]{1,0:T(8,128)(2,1)} %constant.156.clone.dl_ref, f32[16,256]{1,0:T(8,128)} %constant.157.clone.turn_ref), custom_call_target="tpu_custom_call" | custom-call | tf_op jit(solution)/shard_map/second_section/pallas_call | solution.py:209
  45.0 4.4 %all-to-all-start.1 = ((bf16[8,2,144,128]{3,2,1,0:T(8,128)(2,1)}), bf16[8,2,144,128]{3,2,1,0:T(8,128)(2,1)}, u32[]{:S(2)}, u32[]{:S(2)}) async-start(bf16[8,2,144,128]{3,2,1,0:T(8,128)(2,1)} %second_section.1), calls=%async_computation.1 | async-start | bytes 1179648 | tf_op jit(solution)/shard_map/all_to_all | solution.py:240
  50.5 2.6 bitcast_select_fusion
  53.1 1.7 compare_and_fusion
  54.8 5.1 %all-to-all-done.1 = bf16[8,2,144,128]{3,2,1,0:T(8,128)(2,1)} async-done(((bf16[8,2,144,128]{3,2,1,0:T(8,128)(2,1)}), bf16[8,2,144,128]{3,2,1,0:T(8,128)(2,1)}, u32[]{:S(2)}, u32[]{:S(2)}) %all-to-all-start.1) | async-done | bytes 589856 | tf_op jit(solution)/shard_map/all_to_all | solution.py:240
  60.0 1.9 fusion.128
  61.9 0.8 copy.25
  62.7 3.2 rev.3
  65.9 1.1 copy.27
  67.0 1.7 multiply_reduce_fusion.5
  70.5 2.3 multiply_convert_fusion.2
  72.9 0.8 multiply_reduce_fusion.4
  75.7 2.4 multiply_convert_fusion.1
  78.0 1.0 copy-done.30
  79.0 0.8 multiply_reduce_fusion.3
  80.2 1.2 copy-done.10
  82.9 2.4 multiply_convert_fusion
  85.3 1.0 copy-done.21
  87.4 0.8 fusion.12
  88.8 3.8 %all-to-all-start.2 = ((f32[8,8,512]{2,1,0:T(8,128)}), f32[8,8,512]{2,1,0:T(8,128)S(1)}, u32[]{:S(2)}, u32[]{:S(2)}) async-start(f32[8,8,512]{2,1,0:T(8,128)} %broadcast_in_dim.103), calls=%async_computation.2 | async-start | bytes 262144 | tf_op jit(solution)/shard_map/all_to_all | solution.py:268
  92.9 2.1 fusion.94
  95.0 4.4 %all-to-all-done.2 = f32[8,8,512]{2,1,0:T(8,128)S(1)} async-done(((f32[8,8,512]{2,1,0:T(8,128)}), f32[8,8,512]{2,1,0:T(8,128)S(1)}, u32[]{:S(2)}, u32[]{:S(2)}) %all-to-all-start.2) | async-done | bytes 131104 | tf_op jit(solution)/shard_map/all_to_all | solution.py:268
  99.4 0.8 fusion.108
  101.0 3.3 %fusion.6 = bf16[1040,512]{1,0:T(8,128)(2,1)S(1)} fusion(f32[1040,512]{1,0:T(8,128)} %get-tuple-element.60, pred[1040]{0:T(1024)(128)(4,1)S(1)} %fusion.98, bf16[3,512,512]{2,1,0:T(8,128)(2,1)} %param.19, f32[512]{0:T(512)S(1)} %fusion.101, s32[512]{0:T(512)S(1)} %lt.24, s32[512]{0:T(512)S(1)} %ge.27, s32[1040]{0:T(1024)S(1)} %fusion.97), kind=kOutput, calls=%fused_computation.23 | convolution fusion | flops 552714240 | bytes 3730512 | tf_op jit(solution)/shard_map/dot_general | solution.py:234
  104.3 0.8 fusion.21
  105.1 1.7 fusion.40
  106.8 1.8 fusion.44
  109.4 0.9 multiply_reduce_fusion.2
  110.4 1.0 fusion.125
  111.4 1.0 copy-done.32
  112.7 1.3 fusion.7
  114.1 0.8 fusion.18
  115.3 1.7 fusion.46
  117.1 1.7 fusion.48
  118.8 1.7 fusion.50
  120.5 0.8 convolution_add_fusion.3
  121.3 0.8 copy-done.5
  122.1 0.9 multiply_reduce_fusion.1
  123.0 2.7 fusion.127
  125.8 1.3 fusion.8
  127.6 2.1 fusion.15
  129.7 1.7 fusion.52
  131.4 1.8 fusion.54
  133.2 1.7 fusion.56
  134.9 1.8 fusion.42
  136.7 1.4 select_convert_fusion
  138.8 2.5 convolution_add_fusion.1
  141.3 0.9 multiply_reduce_fusion
  144.5 1.3 fusion.13
  147.7 1.2 select_reduce_fusion
  154.4 1.8 convolution_dynamic-update-slice_fusion.2
  156.2 1.7 convolution_dynamic-update-slice_fusion.1
  158.7 1.7 convolution_dynamic-update-slice_fusion
  161.1 153.8 %all-reduce.9.cloned.1.call-done = f32[1952,512]{1,0:T(8,128)} async-done(((f32[1952,512]{1,0:T(8,128)}), f32[1952,512]{1,0:T(8,128)}) %all-reduce.9.cloned.1.call-update) | async-done | bytes 3997712 | tf_op jit(solution)/shard_map/psum | solution.py:321
  315.0 1.2 slice.326
  316.2 1.9 slice.327
  318.0 1.7 slice.328
  319.8 3.9 %slice.329 = f32[1536,512]{1,0:T(8,128)} slice(f32[1952,512]{1,0:T(8,128)} %all-reduce.9.cloned.1.call-done), slice={[400:1936], [0:512]} | slice | bytes 6291456 | tf_op jit(solution)/shard_map/slice | solution.py:329
  323.6 1.4 slice_bitcast_fusion.33
  (146 shorter events, 22.1 us)
Async XLA Ops:
  7.2 59.8 %copy-start = (bf16[256,512]{1,0:T(8,128)(2,1)S(1)}, bf16[256,512]{1,0:T(8,128)(2,1)}, u32[]{:S(2)}) copy-start(bf16[256,512]{1,0:T(8,128)(2,1)} %param.17) | copy-start | bytes 786436
  7.2 15.7 %copy-start.47 = (s32[33]{0:T(128)S(1)}, s32[33]{0:T(128)}, u32[]{:S(2)}) copy-start(s32[33]{0:T(128)} %param.22) | copy-start | bytes 400
  14.5 8.4 %copy-start.45 = (bf16[3,3,16,512]{3,2,1,0:T(8,128)(2,1)S(1)}, bf16[3,3,16,512]{3,2,1,0:T(8,128)(2,1)}, u32[]{:S(2)}) copy-start(bf16[3,3,16,512]{3,2,1,0:T(8,128)(2,1)} %param.18) | copy-start | bytes 442372
  14.5 23.9 %all-to-all-start = ((bf16[8,2,128,256]{3,2,1,0:T(8,128)(2,1)}), bf16[8,2,128,256]{3,2,1,0:T(8,128)(2,1)S(1)}, u32[]{:S(2)}, u32[]{:S(2)}) async-start(bf16[8,2,128,256]{3,2,1,0:T(8,128)(2,1)} %first_section.1), calls=%async_computation | async-start | bytes 2097152 | tf_op jit(solution)/shard_map/all_to_all | solution.py:239
  38.4 1.0 copy-start.20
  45.0 15.0 %all-to-all-start.1 = ((bf16[8,2,144,128]{3,2,1,0:T(8,128)(2,1)}), bf16[8,2,144,128]{3,2,1,0:T(8,128)(2,1)}, u32[]{:S(2)}, u32[]{:S(2)}) async-start(bf16[8,2,144,128]{3,2,1,0:T(8,128)(2,1)} %second_section.1), calls=%async_computation.1 | async-start | bytes 1179648 | tf_op jit(solution)/shard_map/all_to_all | solution.py:240
  53.1 17.4 %copy-start.6 = (bf16[3,512,512]{2,1,0:T(8,128)(2,1)}, bf16[3,512,512]{2,1,0:T(8,128)(2,1)S(1)}, u32[]{:S(2)}) copy-start(bf16[3,512,512]{2,1,0:T(8,128)(2,1)S(1)} %get-tuple-element.36) | copy-start | bytes 4718596
  53.1 22.6 %copy-start.8 = (bf16[3,512,512]{2,1,0:T(8,128)(2,1)}, bf16[3,512,512]{2,1,0:T(8,128)(2,1)S(1)}, u32[]{:S(2)}) copy-start(bf16[3,512,512]{2,1,0:T(8,128)(2,1)S(1)} %get-tuple-element.35) | copy-start | bytes 4718596
  66.9 1.7 copy-start.23
  68.6 4.2 %copy-start.2 = (f32[1040,512]{1,0:T(8,128)}, f32[1040,512]{1,0:T(8,128)S(1)}, u32[]{:S(2)}) copy-start(f32[1040,512]{1,0:T(8,128)S(1)} %get-tuple-element.50) | copy-start | bytes 6389764
  69.0 1.5 copy-start.12
  70.5 2.4 copy-start.25
  72.8 1.0 copy-start.28
  73.8 4.2 %copy-start.4 = (f32[1040,512]{1,0:T(8,128)}, f32[1040,512]{1,0:T(8,128)S(1)}, u32[]{:S(2)}) copy-start(f32[1040,512]{1,0:T(8,128)S(1)} %get-tuple-element.54) | copy-start | bytes 6389764
  74.2 1.5 copy-start.16
  78.0 1.0 copy-start.30
  79.9 1.6 copy-start.10
  80.2 26.6 %copy-start.14 = (bf16[1040,512]{1,0:T(8,128)(2,1)}, bf16[1040,512]{1,0:T(8,128)(2,1)S(1)}, u32[]{:S(2)}) copy-start(bf16[1040,512]{1,0:T(8,128)(2,1)S(1)} %select_convert_fusion.1) | copy-start | bytes 3194884
  85.3 1.0 copy-start.21
  86.3 1.0 copy-start.24
  87.4 12.0 %copy-start.46 = (f32[512,10]{0,1:T(8,128)S(1)}, f32[512,10]{0,1:T(8,128)}, u32[]{:S(2)}) copy-start(f32[512,10]{0,1:T(8,128)} %param.20) | copy-start | bytes 61444
  88.8 10.6 %all-to-all-start.2 = ((f32[8,8,512]{2,1,0:T(8,128)}), f32[8,8,512]{2,1,0:T(8,128)S(1)}, u32[]{:S(2)}, u32[]{:S(2)}) async-start(f32[8,8,512]{2,1,0:T(8,128)} %broadcast_in_dim.103), calls=%async_computation.2 | async-start | bytes 262144 | tf_op jit(solution)/shard_map/all_to_all | solution.py:268
  92.6 222.4 %all-reduce.9.cloned.1.call-start = ((), (), s32[]{:S(2)}) async-start(), calls=%async_computation.3 | async-start | bytes 7995392 | tf_op jit(solution)/shard_map/psum | solution.py:321
  101.0 3.4 %copy-start.11 = (bf16[3,512,512]{2,1,0:T(8,128)(2,1)S(1)}, bf16[3,512,512]{2,1,0:T(8,128)(2,1)}, u32[]{:S(2)}) copy-start(bf16[3,512,512]{2,1,0:T(8,128)(2,1)} %get-tuple-element.34) | copy-start | bytes 4718596
  110.4 2.0 copy-start.26
  110.4 2.3 copy-start.49
  111.4 1.0 copy-start.32
  112.7 1.4 copy-start.9
  114.1 1.2 copy-start.17
  120.5 1.6 copy-start.5
  123.0 2.8 copy-start.48
  125.8 1.3 copy-start.34
  125.8 1.8 copy-start.7
  127.6 2.1 copy-start.13
  133.2 1.7 copy-start.15
  138.8 2.5 copy-start.3
  141.3 1.6 copy-start.18
  142.9 1.0 copy-start.19
  142.9 2.8 copy-start.44
  144.0 1.8 copy-start.41
  144.0 1.8 copy-start.42
  144.0 1.9 copy-start.43
  144.4 2.0 copy-start.36
  144.4 2.3 copy-start.37
  144.4 2.6 copy-start.38
  144.5 2.9 copy-start.39
  144.5 3.2 copy-start.40
  147.7 6.8 %copy-start.29 = (bf16[1040,512]{1,0:T(8,128)(2,1)S(1)}, bf16[1040,512]{1,0:T(8,128)(2,1)}, u32[]{:S(2)}) copy-start(bf16[1040,512]{1,0:T(8,128)(2,1)} %copy-done.28) | copy-start | bytes 3194884
  147.7 6.8 %copy-start.35 = (bf16[1040,512]{1,0:T(8,128)(2,1)S(1)}, bf16[1040,512]{1,0:T(8,128)(2,1)}, u32[]{:S(2)}) copy-start(bf16[1040,512]{1,0:T(8,128)(2,1)} %copy-done.34) | copy-start | bytes 3194884
  154.4 1.8 copy-start.31
  154.4 1.8 copy-start.33
  156.2 2.5 copy-start.22
  156.2 2.5 copy-start.27
  318.0 7.0 %copy-start.1 = (bf16[256,512]{1,0:T(8,128)(2,1)S(1)}, bf16[256,512]{1,0:T(8,128)(2,1)}, u32[]{:S(2)}) copy-start(bf16[256,512]{1,0:T(8,128)(2,1)} %param.17) | copy-start | bytes 786436
Sparse Core Ops, SparseCore 0:
  161.2 153.6 all-reduce.8

commit v2 on v1

--- a/solution.py
+++ b/solution.py
@@ -99,8 +99,8 @@
             )
         real = parts[0][:128] + sign * parts[1][128:]
         imag = parts[0][128:] - sign * parts[1][:128]
-        out_ref[channel, 0] = (real * cosine - imag * sine).astype(BF16)
-        out_ref[channel, 1] = (real * sine + imag * cosine).astype(BF16)
+        out_ref[channel, 0] = real * cosine - imag * sine
+        out_ref[channel, 1] = real * sine + imag * cosine
 
 
 def first_section(records):
@@ -109,7 +109,7 @@
     return pl.pallas_call(
         first_kernel,
         grid=(4,),
-        out_shape=jax.ShapeDtypeStruct((PARTS, 2, 128, COLS), BF16),
+        out_shape=jax.ShapeDtypeStruct((PARTS, 2, 128, COLS), F32),
         in_specs=[
             pl.BlockSpec((2, N1, COLS), lambda j: (0, 0, 0)),
             pl.BlockSpec((256, 512), lambda j: (j, 0)),
@@ -156,7 +156,7 @@
     def step(index, carry):
         rows = pl.ds(pl.multiple_of(index * rows_at_once, rows_at_once), rows_at_once)
         values = [
-            (load(part, 0, rows).astype(F32), load(part, 1, rows).astype(F32))
+            (load(part, 0, rows), load(part, 1, rows))
             for part in range(PARTS)
         ]
         for u, (real, imag) in enumerate(eight_point(values)):
@@ -216,6 +216,188 @@
         ],
         name="second_section",
     )(exchanged, jnp.asarray(table_high), jnp.asarray(table_low), jnp.asarray(turn))
+
+
+MESH = pl.DeviceIdType.MESH
+SIDE = 4
+PART_ROWS = (1536, 1536, 512)
+PART_LANES = (128, 128, 256)
+PART_AXES = ((0, 1, 2), (1, 2, 0), (2, 0, 1))
+STEM_ROWS, CONV_ROWS, REST_ROWS = 256, 144, 16
+
+
+def reduce_kernel(
+    mix_ref, stem_ref, conv_ref, rest_ref, mix_out, stem_out, conv_out, rest_out, *scratch
+):
+    acc = scratch[0:3]
+    pair = scratch[3:6]
+    full = scratch[6:9]
+    landing = [scratch[9 + 3 * part : 12 + 3 * part] for part in range(3)]
+    pair_send, pair_recv, send, recv = scratch[18:22]
+    dp, freq = lax.axis_index("dp"), lax.axis_index("freq")
+    core = dp % 2
+    spot = (freq // 2, dp // 4, (freq % 2) * 2 + (dp // 2) % 2)
+
+    def device(place, which):
+        x, y, z = place
+        return {"dp": (y * 2 + z % 2) * 2 + which, "freq": x * 2 + z // 2}
+
+    def neighbour(axis, distance):
+        place = list(spot)
+        place[axis] = (spot[axis] + distance) % SIDE
+        return device(place, core), place[axis]
+
+    partner = device(spot, 1 - core)
+    barrier = pltpu.get_barrier_semaphore()
+    pl.semaphore_signal(barrier, inc=1, device_id=partner, device_id_type=MESH)
+    for axis in range(3):
+        for distance in range(1, SIDE):
+            pl.semaphore_signal(
+                barrier, inc=1, device_id=neighbour(axis, distance)[0], device_id_type=MESH
+            )
+    pl.semaphore_wait(barrier, 10)
+
+    def lanes(owner, start, size):
+        return pl.ds(pl.multiple_of(owner * 256 + start, 128), size)
+
+    def pieces(mix, stem, conv, rest):
+        first = STEM_ROWS + CONV_ROWS
+        return (
+            (0, mix, 0, 128, slice(0, 1536)),
+            (1, mix, 128, 128, slice(0, 1536)),
+            (2, stem, 0, 256, slice(0, STEM_ROWS)),
+            (2, conv, 0, 256, slice(STEM_ROWS, first)),
+            (2, rest, 0, 256, slice(first, first + REST_ROWS)),
+        )
+
+    inputs = pieces(mix_ref, stem_ref, conv_ref, rest_ref)
+    outputs = pieces(mix_out, stem_out, conv_out, rest_out)
+    copies = []
+    for index, (part, ref, start, size, rows) in enumerate(inputs):
+        copies.append(
+            pltpu.make_async_remote_copy(
+                src_ref=ref.at[:, lanes(1 - core, start, size)],
+                dst_ref=pair[part].at[rows, :],
+                send_sem=pair_send.at[0, index],
+                recv_sem=pair_recv.at[0, index],
+                device_id=partner,
+                device_id_type=MESH,
+            )
+        )
+        copies[-1].start()
+    used = STEM_ROWS + CONV_ROWS + REST_ROWS
+    acc[2][used:, :] = jnp.zeros((PART_ROWS[2] - used, PART_LANES[2]), F32)
+
+    counts = [[rows // SIDE ** (stage + 1) for stage in range(3)] for rows in PART_ROWS]
+    offsets = []
+    for part in range(3):
+        chain = [0]
+        for stage in range(3):
+            chain.append(chain[-1] + spot[PART_AXES[part][stage]] * counts[part][stage])
+        offsets.append(chain)
+
+    def window(part, start, stage):
+        return pl.ds(pl.multiple_of(start, 8), counts[part][stage])
+
+    def scatter(part, stage):
+        started = []
+        for distance in range(1, SIDE):
+            target, coordinate = neighbour(PART_AXES[part][stage], distance)
+            start = offsets[part][stage] + coordinate * counts[part][stage]
+            started.append(
+                pltpu.make_async_remote_copy(
+                    src_ref=acc[part].at[window(part, start, stage), :],
+                    dst_ref=landing[part][stage].at[distance - 1],
+                    send_sem=send.at[part, stage, distance - 1],
+                    recv_sem=recv.at[part, stage, distance - 1],
+                    device_id=target,
+                    device_id_type=MESH,
+                )
+            )
+            started[-1].start()
+        return started
+
+    def gather(part, stage):
+        started = []
+        rows = window(part, offsets[part][stage + 1], stage)
+        for distance in range(1, SIDE):
+            target, _ = neighbour(PART_AXES[part][stage], distance)
+            started.append(
+                pltpu.make_async_remote_copy(
+                    src_ref=full[part].at[rows, :],
+                    dst_ref=full[part].at[rows, :],
+                    send_sem=send.at[part, 3 + stage, distance - 1],
+                    recv_sem=recv.at[part, 3 + stage, distance - 1],
+                    device_id=target,
+                    device_id_type=MESH,
+                )
+            )
+            started[-1].start()
+        return started
+
+    flying = [None] * 3
+    for index, (part, ref, start, size, rows) in enumerate(inputs):
+        copies[index].wait()
+        acc[part][rows, :] = ref[:, lanes(core, start, size)] + pair[part][rows, :]
+        if index != 2 and index != 3:
+            flying[part] = scatter(part, 0)
+    for stage in range(3):
+        for part in range(3):
+            for copy in flying[part]:
+                copy.wait()
+            rows = window(part, offsets[part][stage + 1], stage)
+            arrived = landing[part][stage]
+            total = acc if stage < 2 else full
+            total[part][rows, :] = (acc[part][rows, :] + arrived[0]) + (arrived[1] + arrived[2])
+            flying[part] = scatter(part, stage + 1) if stage < 2 else gather(part, 2)
+    for stage in (1, 0):
+        for part in range(3):
+            for copy in flying[part]:
+                copy.wait()
+            flying[part] = gather(part, stage)
+    last = []
+    for index, (part, ref, start, size, rows) in enumerate(outputs):
+        if index < 3:
+            for copy in flying[part]:
+                copy.wait()
+        last.append(
+            pltpu.make_async_remote_copy(
+                src_ref=full[part].at[rows, :],
+                dst_ref=ref.at[:, lanes(core, start, size)],
+                send_sem=pair_send.at[1, index],
+                recv_sem=pair_recv.at[1, index],
+                device_id=partner,
+                device_id_type=MESH,
+            )
+        )
+        last[-1].start()
+        ref[:, lanes(core, start, size)] = full[part][rows, :]
+    for copy in last:
+        copy.wait()
+
+
+def reduce_everywhere(mix, stem, conv, rest):
+    buffers = [pltpu.VMEM((rows, width), F32) for rows, width in zip(PART_ROWS, PART_LANES)]
+    landing = [
+        pltpu.VMEM((SIDE - 1, rows // SIDE ** (stage + 1), width), F32)
+        for rows, width in zip(PART_ROWS, PART_LANES)
+        for stage in range(3)
+    ]
+    arrays = (mix, stem, conv, rest)
+    return pl.pallas_call(
+        reduce_kernel,
+        out_shape=[jax.ShapeDtypeStruct(a.shape, F32) for a in arrays],
+        in_specs=[pl.BlockSpec(memory_space=pltpu.VMEM)] * 4,
+        out_specs=[pl.BlockSpec(memory_space=pltpu.VMEM)] * 4,
+        scratch_shapes=buffers
+        + buffers
+        + buffers
+        + landing
+        + [pltpu.SemaphoreType.DMA((2, 5))] * 2
+        + [pltpu.SemaphoreType.DMA((3, 6, 3))] * 2,
+        compiler_params=pltpu.CompilerParams(collective_id=0, has_side_effects=True),
+        name="reduce_everywhere",
+    )(*arrays)
 
 
 def group_mask(channels):
@@ -315,19 +497,16 @@
     grad_stem = matmul(own_positions, grad_high[own], ((0,), (0,))) + matmul(
         own_positions, grad_low[own], ((0,), (0,))
     )
-    pieces = [grad_stem] + conv_grads + mix_grads + [
-        jnp.pad(head_part, ((0, 16 - classes), (0, 0))).at[15, 0].set(loss)
-    ]
-    packed = lax.psum(jnp.concatenate(pieces, axis=0), ("dp", "freq"))
-    stem_rows = positions.shape[1]
-    conv_rows = stem_rows + layers * KW * GROUP_WIDTH
-    mix_rows = conv_rows + layers * channels
+    rest = jnp.pad(head_part, ((0, REST_ROWS - classes), (0, 0))).at[REST_ROWS - 1, 0].set(loss)
+    mix_all, stem_all, conv_all, rest_all = reduce_everywhere(
+        jnp.concatenate(mix_grads, axis=0), grad_stem, jnp.concatenate(conv_grads, axis=0), rest
+    )
     return (
-        packed[mix_rows + 15, 0],
-        packed[:stem_rows],
-        packed[stem_rows:conv_rows].reshape(layers, KW, GROUP_WIDTH, channels),
-        packed[conv_rows:mix_rows].reshape(layers, channels, channels),
-        packed[mix_rows : mix_rows + classes].T,
+        rest_all[REST_ROWS - 1, 0],
+        stem_all,
+        conv_all.reshape(layers, KW, GROUP_WIDTH, channels),
+        mix_all.reshape(layers, channels, channels),
+        rest_all[:classes].T,
     )
 
 

time: 333 us -> 239 us (0.72); the launches traced: 332 us -> 234 us
  waiting for transfers between devices: 177 us -> 37.7 us
  Pallas kernels: 12.9 us -> 66.1 us
  between operations: 16.6 us -> 3.75 us
  local copies, waits for them, and re-layouts: 35.9 us -> 30.1 us
  other arithmetic: 17.1 us -> 21.5 us
    psum x1 -> x0, waiting for transfers between devices: 154 us -> none  [local(): packed = lax.psum(jnp.concatenate(pieces, axis=0), ('dp', 'freq'))]
    pallas_call x0 -> x1, Pallas kernels: none -> 52.7 us  [reduce_everywhere(): pl.pallas_call(reduce_kernel, out_shape=[jax.ShapeDtypeStruct(a.shape, F3...]
    all_to_all x1, waiting for transfers between devices: 13.9 us -> 28.9 us  [local(): lax.all_to_all(first_section(records[0]), 'freq', 0, 0, tiled=True)]
    slice x4 -> x1, local copies, waits for them, and re-layouts: 8.65 us -> 1.19 us  [local(): rest_all[REST_ROWS - 1, 0]]
    unnamed x111 -> x113, local copies, waits for them, and re-layouts: 18.4 us -> 20.6 us
  transfers between devices with their start and end apart: 4 -> 3, of which waited for: 4 -> 3; matrix products, arithmetic and copies ran while one was open for 3% -> 4% of each run, Pallas kernels for 0% -> 0%
where the time goes in v2:
time: 239 us; the launch traced here: 234 us
  Pallas kernels  66.1 us (28%)
  matrix products  57.3 us (24%)
  waiting for transfers between devices  37.7 us (16%)
  local copies, waits for them, and re-layouts  30.1 us (13%)
  other arithmetic  21.5 us (9%)
  starting transfers between devices  17.9 us (7%)
  between operations  3.75 us (2%)
    dot_general x39, matrix products, matmul(): return lax.dot_general(a, b, (dims, ((), ())), preferred_element_type=F32)  56.4 us
    pallas_call x1, Pallas kernels, reduce_everywhere(): pl.pallas_call(reduce_kernel, out_shape=[jax.ShapeDtypeStruct(a.shape, F3...  52.7 us
    all_to_all x1, waiting for transfers between devices, local(): lax.all_to_all(first_section(records[0]), 'freq', 0, 0, tiled=True)  28.9 us
    unnamed x113, local copies, waits for them, and re-layouts  20.6 us
    all_to_all x1, starting transfers between devices, local(): lax.all_to_all(first_section(records[0]), 'freq', 0, 0, tiled=True)  8.29 us
    pallas_call x1, Pallas kernels, first_section(): pl.pallas_call(first_kernel, grid=(4,), out_shape=jax.ShapeDtypeStruct((P...  7.52 us
    pallas_call x1, Pallas kernels, second_section(): pl.pallas_call(second_kernel, out_shape=jax.ShapeDtypeStruct((PARTS, 2, B...  5.87 us
    convert_element_type x3, other arithmetic, local(): grad_out = grad_stream.astype(BF16)  5.35 us
  transfers between devices with their start and end apart: 3, of which 3 were waited for; matrix products, arithmetic and copies ran while one was open for 4% of the time, Pallas kernels for 0%

profile of v2, /device:TPU:1, one launch (start us, length us, event | category | flops | bytes accessed | tf_op | source)
XLA Modules:
  0.0 234.3 jit_solution(235602805569802601)
XLA Ops:
  0.6 7.5 %first_section.1 = f32[8,2,128,256]{3,2,1,0:T(8,128)} custom-call(f32[2,1024,256]{2,1,0:T(8,128)} %bitcast.146, bf16[1024,512]{1,0:T(8,128)(2,1)} %constant.151.clone.th_ref, bf16[1024,512]{1,0:T(8,128)(2,1)} %constant.152.clone.tl_ref, f32[2,512,256]{2,1,0:T(8,128)} %constant.153.clone.turn_ref, f32[512,16]{1,0:T(8,128)} %constant.154.clone.own_ref), custom_call_target="tpu_custom_call" | custom-call | tf_op jit(solution)/shard_map/first_section/pallas_call | solution.py:109
  8.2 8.3 %all-to-all-start = ((f32[8,2,128,256]{3,2,1,0:T(8,128)}), f32[8,2,128,256]{3,2,1,0:T(8,128)S(1)}, u32[]{:S(2)}, u32[]{:S(2)}) async-start(f32[8,2,128,256]{3,2,1,0:T(8,128)} %first_section.1), calls=%async_computation | async-start | bytes 4194304 | tf_op jit(solution)/shard_map/all_to_all | solution.py:421
  17.2 1.0 select_compare_fusion.1
  18.2 28.9 %all-to-all-done.x_ref = f32[8,2,128,256]{3,2,1,0:T(8,128)S(1)} async-done(((f32[8,2,128,256]{3,2,1,0:T(8,128)}), f32[8,2,128,256]{3,2,1,0:T(8,128)S(1)}, u32[]{:S(2)}, u32[]{:S(2)}) %all-to-all-start) | async-done | bytes 2097184 | tf_op jit(solution)/shard_map/all_to_all | solution.py:421
  47.1 1.3 copy-done.19
  48.4 5.9 %second_section.1 = bf16[8,2,144,128]{3,2,1,0:T(8,128)(2,1)} custom-call(f32[8,2,128,256]{3,2,1,0:T(8,128)} %copy-done.19, bf16[512,512]{1,0:T(8,128)(2,1)} %constant.155.clone.dh_ref, bf16[512,512]{1,0:T(8,128)(2,1)} %constant.156.clone.dl_ref, f32[16,256]{1,0:T(8,128)} %constant.157.clone.turn_ref), custom_call_target="tpu_custom_call" | custom-call | tf_op jit(solution)/shard_map/second_section/pallas_call | solution.py:209
  54.3 4.4 %all-to-all-start.1 = ((bf16[8,2,144,128]{3,2,1,0:T(8,128)(2,1)}), bf16[8,2,144,128]{3,2,1,0:T(8,128)(2,1)}, u32[]{:S(2)}, u32[]{:S(2)}) async-start(bf16[8,2,144,128]{3,2,1,0:T(8,128)(2,1)} %second_section.1), calls=%async_computation.1 | async-start | bytes 1179648 | tf_op jit(solution)/shard_map/all_to_all | solution.py:422
  59.8 2.6 %bitcast_select_fusion = (bf16[3,512,512]{2,1,0:T(8,128)(2,1)}, bf16[3,512,512]{2,1,0:T(8,128)(2,1)S(1)}, bf16[3,512,512]{2,1,0:T(8,128)(2,1)S(1)}) fusion(pred[512,512]{1,0:T(8,128)(4,1)} %select_compare_fusion.1, bf16[3,16,512]{2,1,0:T(8,128)(2,1)S(1)} %get-tuple-element.45, bf16[3,16,512]{2,1,0:T(8,128)(2,1)} %get-tuple-element.47, ...), kind=kLoop, calls=%fused_computation.54 | loop fusion | flops 2359296 | bytes 5128192 | tf_op jit(solution)/shard_map/jit(_where)/select_n | solution.py:412
  62.4 1.7 compare_and_fusion
  64.0 4.2 %all-to-all-done.1 = bf16[8,2,144,128]{3,2,1,0:T(8,128)(2,1)} async-done(((bf16[8,2,144,128]{3,2,1,0:T(8,128)(2,1)}), bf16[8,2,144,128]{3,2,1,0:T(8,128)(2,1)}, u32[]{:S(2)}, u32[]{:S(2)}) %all-to-all-start.1) | async-done | bytes 589856 | tf_op jit(solution)/shard_map/all_to_all | solution.py:422
  68.3 1.9 fusion.130
  70.2 0.8 copy.25
  71.0 3.2 %rev.3 = bf16[4,2,1,130,128]{4,0,1,3,2:T(4,128)(2,1)} reverse(bf16[4,2,1,130,128]{4,0,1,3,2:T(4,128)(2,1)} %copy.25), dimensions={0} | reverse | bytes 532480 | tf_op jit(solution)/shard_map/rev | solution.py:426
  74.2 1.1 copy.27
  75.3 1.7 multiply_reduce_fusion.5
  78.8 2.3 multiply_convert_fusion.2
  81.2 0.8 multiply_reduce_fusion.4
  84.0 2.4 %multiply_convert_fusion.1 = (bf16[1040,512]{1,0:T(8,128)(2,1)S(1)}, f32[1040,512]{1,0:T(8,128)}) fusion(f32[1040,512]{1,0:T(8,128)S(1)} %convolution_add_fusion.10, bf16[3,512,512]{2,1,0:T(8,128)(2,1)S(1)} %get-tuple-element.43, bf16[1040,512]{1,0:T(8,128)(2,1)S(1)} %select_convert_fusion.2), kind=kOutput, calls=%fused_computation.39 | convolution fusion | flops 548454400 | bytes 6914048 | tf_op jit(solution)/shard_map/dot_general | solution.py:416
  86.3 1.0 copy-done.29
  87.3 0.8 multiply_reduce_fusion.3
  88.5 1.2 copy-done.10
  91.2 2.4 %multiply_convert_fusion = (bf16[1040,512]{1,0:T(8,128)(2,1)S(1)}, f32[1040,512]{1,0:T(8,128)}) fusion(f32[1040,512]{1,0:T(8,128)S(1)} %convolution_add_fusion.7, bf16[3,512,512]{2,1,0:T(8,128)(2,1)S(1)} %copy-done.10, bf16[1040,512]{1,0:T(8,128)(2,1)S(1)} %select_convert_fusion.1), kind=kOutput, calls=%fused_computation.35 | convolution fusion | flops 548454400 | bytes 6914048 | tf_op jit(solution)/shard_map/dot_general | solution.py:416
  93.6 1.0 copy-done.21
  97.1 5.2 %all-to-all-start.2 = ((f32[8,8,512]{2,1,0:T(8,128)}), f32[8,8,512]{2,1,0:T(8,128)S(1)}, u32[]{:S(2)}, u32[]{:S(2)}) async-start(f32[8,8,512]{2,1,0:T(8,128)} %broadcast_in_dim.103), calls=%async_computation.2 | async-start | bytes 262144 | tf_op jit(solution)/shard_map/all_to_all | solution.py:450
  102.3 2.1 fusion.96
  104.4 4.6 %all-to-all-done.2 = f32[8,8,512]{2,1,0:T(8,128)S(1)} async-done(((f32[8,8,512]{2,1,0:T(8,128)}), f32[8,8,512]{2,1,0:T(8,128)S(1)}, u32[]{:S(2)}, u32[]{:S(2)}) %all-to-all-start.2) | async-done | bytes 131104 | tf_op jit(solution)/shard_map/all_to_all | solution.py:450
  110.7 1.4 select_convert_fusion
  112.1 3.3 %fusion.6 = bf16[1040,512]{1,0:T(8,128)(2,1)S(1)} fusion(f32[1040,512]{1,0:T(8,128)} %get-tuple-element.68, pred[1040]{0:T(1024)(128)(4,1)S(1)} %fusion.100, bf16[3,512,512]{2,1,0:T(8,128)(2,1)} %param.19, f32[512]{0:T(512)S(1)} %fusion.103, s32[512]{0:T(512)S(1)} %lt.26, s32[512]{0:T(512)S(1)} %ge.29, s32[1040]{0:T(1024)S(1)} %fusion.97), kind=kOutput, calls=%fused_computation.24 | convolution fusion | flops 552714240 | bytes 3730512 | tf_op jit(solution)/shard_map/dot_general | solution.py:416
  115.4 0.8 fusion.20
  116.2 1.7 fusion.33
  117.9 1.8 fusion.37
  120.5 0.9 multiply_reduce_fusion.2
  121.4 1.0 fusion.127
  122.7 1.7 fusion.54
  125.1 1.3 fusion.7
  127.7 1.7 fusion.39
  129.5 1.7 fusion.41
  131.2 1.7 fusion.43
  133.0 0.8 convolution_add_fusion.3
  133.8 0.8 copy-done.5
  134.6 0.9 multiply_reduce_fusion.1
  135.5 3.0 %fusion.129 = (bf16[1040,512]{1,0:T(8,128)(2,1)S(1)}, f32[1040,512]{1,0:T(8,128)}) fusion(f32[1040]{0:T(1024)S(1)} %broadcast_multiply_fusion.1, f32[1040,512]{1,0:T(8,128)S(1)} %copy-done.5, f32[1040]{0:T(1024)S(1)} %get-tuple-element.50, f32[1040,512]{1,0:T(8,128)S(1)} %get-tuple-element.73, f32[1040]{0:T(1024)S(1)} %get-tuple-element.51, ...), kind=kLoop, calls=%fused_computation.240 | loop fusion | flops 7987200 | bytes 11749824 | tf_op jit(solution)/shard_map/convert_element_type | solution.py:471
  138.4 1.7 fusion.57
  140.2 1.3 fusion.8
  141.5 3.2 %fusion.14 = f32[1040,512]{1,0:T(8,128)} fusion(bf16[1040,512]{1,0:T(8,128)(2,1)S(1)} %fusion.8, bf16[3,512,512]{2,1,0:T(8,128)(2,1)} %copy-done.6), kind=kOutput, calls=%fused_computation.60 | convolution fusion | flops 545259520 | bytes 3719168 | tf_op jit(solution)/shard_map/dot_general | solution.py:416
  144.7 1.8 fusion.45
  146.5 1.7 fusion.47
  148.2 1.7 fusion.49
  149.9 1.7 fusion.35
  152.4 3.1 %fusion.51 = f32[512,512]{1,0:T(8,128)} fusion(bf16[1040,512]{1,0:T(8,128)(2,1)} %select_convert_fusion, bf16[1040,512]{1,0:T(8,128)(2,1)S(1)} %copy-done.22), kind=kOutput, calls=%fused_computation.96 | convolution fusion | flops 536870912 | bytes 3145728 | tf_op jit(solution)/shard_map/dot_general | solution.py:416
  155.6 0.8 convolution_add_fusion.1
  156.4 0.8 copy-done.3
  157.2 2.2 multiply_reduce_fusion
  159.4 0.8 copy-done.34
  161.1 1.2 select_reduce_fusion
  163.1 2.9 %fusion.128 = (f32[1040,512]{1,0:T(8,128)S(1)}, f32[1040,512]{1,0:T(8,128)S(1)}) fusion(f32[1040]{0:T(1024)S(1)} %broadcast_multiply_fusion, f32[1040,512]{1,0:T(8,128)S(1)} %copy-done.3, f32[1040]{0:T(1024)S(1)} %get-tuple-element.48, f32[1040,512]{1,0:T(8,128)} %get-tuple-element.39, f32[1040,512]{1,0:T(8,128)} %get-tuple-element.75, ...), kind=kLoop, calls=%fused_computation.239 | loop fusion | flops 3194880 | bytes 10662080 | tf_op jit(solution)/shard_map/reduce_precision | solution.py:493
  166.5 1.3 convolution_add_fusion.14.stem_ref
  168.5 2.0 pad_maximum_fusion.mix_ref
  171.1 52.7 %reduce_everywhere.1 = (f32[1536,512]{1,0:T(8,128)}, f32[256,512]{1,0:T(8,128)}, f32[144,512]{1,0:T(8,128)}, f32[16,512]{1,0:T(8,128)}) custom-call(f32[1536,512]{1,0:T(8,128)} %pad_maximum_fusion.mix_ref, f32[256,512]{1,0:T(8,128)} %convolution_add_fusion.14.stem_ref, f32[144,512]{1,0:T(8,128)} %copy-done.43, f32[16,512]{1,0:T(8,128)} %copy-done.45), custom_call_target="tpu_custom_call" | custom-call | tf_op jit(solution)/shard_map/reduce_everywhere/pallas_call | solution.py:387
  223.9 1.2 slice.275
  225.1 1.4 slice_bitcast_fusion.33
  226.4 1.9 copy.41
  228.3 1.7 copy.42
  230.0 3.9 %copy.43 = f32[3,512,512]{2,1,0:T(8,128)} copy(f32[3,512,512]{2,1,0:T(8,128)} %bitcast.141) | data formatting | bytes 6291456
  (144 shorter events, 16.7 us)
Async XLA Ops:
  0.6 74.7 %copy-start = (bf16[256,512]{1,0:T(8,128)(2,1)S(1)}, bf16[256,512]{1,0:T(8,128)(2,1)}, u32[]{:S(2)}) copy-start(bf16[256,512]{1,0:T(8,128)(2,1)} %param.17) | copy-start | bytes 786436
  8.2 8.3 %copy-start.47 = (s32[33]{0:T(128)S(1)}, s32[33]{0:T(128)}, u32[]{:S(2)}) copy-start(s32[33]{0:T(128)} %param.22) | copy-start | bytes 400
  8.2 8.4 %copy-start.44 = (bf16[3,3,16,512]{3,2,1,0:T(8,128)(2,1)S(1)}, bf16[3,3,16,512]{3,2,1,0:T(8,128)(2,1)}, u32[]{:S(2)}) copy-start(bf16[3,3,16,512]{3,2,1,0:T(8,128)(2,1)} %param.18) | copy-start | bytes 442372
  8.2 38.9 %all-to-all-start = ((f32[8,2,128,256]{3,2,1,0:T(8,128)}), f32[8,2,128,256]{3,2,1,0:T(8,128)S(1)}, u32[]{:S(2)}, u32[]{:S(2)}) async-start(f32[8,2,128,256]{3,2,1,0:T(8,128)} %first_section.1), calls=%async_computation | async-start | bytes 4194304 | tf_op jit(solution)/shard_map/all_to_all | solution.py:421
  47.1 1.3 copy-start.19
  54.3 14.0 %all-to-all-start.1 = ((bf16[8,2,144,128]{3,2,1,0:T(8,128)(2,1)}), bf16[8,2,144,128]{3,2,1,0:T(8,128)(2,1)}, u32[]{:S(2)}, u32[]{:S(2)}) async-start(bf16[8,2,144,128]{3,2,1,0:T(8,128)(2,1)} %second_section.1), calls=%async_computation.1 | async-start | bytes 1179648 | tf_op jit(solution)/shard_map/all_to_all | solution.py:422
  62.4 16.4 %copy-start.6 = (bf16[3,512,512]{2,1,0:T(8,128)(2,1)}, bf16[3,512,512]{2,1,0:T(8,128)(2,1)S(1)}, u32[]{:S(2)}) copy-start(bf16[3,512,512]{2,1,0:T(8,128)(2,1)S(1)} %get-tuple-element.44) | copy-start | bytes 4718596
  62.4 21.6 %copy-start.8 = (bf16[3,512,512]{2,1,0:T(8,128)(2,1)}, bf16[3,512,512]{2,1,0:T(8,128)(2,1)S(1)}, u32[]{:S(2)}) copy-start(bf16[3,512,512]{2,1,0:T(8,128)(2,1)S(1)} %get-tuple-element.43) | copy-start | bytes 4718596
  75.3 1.7 copy-start.23
  77.0 4.2 %copy-start.2 = (f32[1040,512]{1,0:T(8,128)}, f32[1040,512]{1,0:T(8,128)S(1)}, u32[]{:S(2)}) copy-start(f32[1040,512]{1,0:T(8,128)S(1)} %get-tuple-element.58) | copy-start | bytes 6389764
  77.3 1.5 copy-start.12
  78.8 2.3 copy-start.25
  81.2 1.0 copy-start.27
  82.1 4.2 %copy-start.4 = (f32[1040,512]{1,0:T(8,128)}, f32[1040,512]{1,0:T(8,128)S(1)}, u32[]{:S(2)}) copy-start(f32[1040,512]{1,0:T(8,128)S(1)} %get-tuple-element.62) | copy-start | bytes 6389764
  82.5 1.5 copy-start.16
  86.3 1.0 copy-start.29
  88.1 1.6 copy-start.10
  88.5 29.4 %copy-start.14 = (bf16[1040,512]{1,0:T(8,128)(2,1)}, bf16[1040,512]{1,0:T(8,128)(2,1)S(1)}, u32[]{:S(2)}) copy-start(bf16[1040,512]{1,0:T(8,128)(2,1)S(1)} %select_convert_fusion.1) | copy-start | bytes 3194884
  93.6 1.0 copy-start.21
  94.6 1.0 copy-start.24
  95.7 13.4 %copy-start.46 = (f32[512,10]{0,1:T(8,128)S(1)}, f32[512,10]{0,1:T(8,128)}, u32[]{:S(2)}) copy-start(f32[512,10]{0,1:T(8,128)} %param.20) | copy-start | bytes 61444
  97.1 11.9 %all-to-all-start.2 = ((f32[8,8,512]{2,1,0:T(8,128)}), f32[8,8,512]{2,1,0:T(8,128)S(1)}, u32[]{:S(2)}, u32[]{:S(2)}) async-start(f32[8,8,512]{2,1,0:T(8,128)} %broadcast_in_dim.103), calls=%async_computation.2 | async-start | bytes 262144 | tf_op jit(solution)/shard_map/all_to_all | solution.py:450
  112.1 3.3 %copy-start.11 = (bf16[3,512,512]{2,1,0:T(8,128)(2,1)S(1)}, bf16[3,512,512]{2,1,0:T(8,128)(2,1)}, u32[]{:S(2)}) copy-start(bf16[3,512,512]{2,1,0:T(8,128)(2,1)} %get-tuple-element.42) | copy-start | bytes 4718596
  121.4 1.2 copy-start.30
  122.7 1.7 copy-start.26
  122.7 2.5 %copy-start.49 = (f32[1040,512]{1,0:T(8,128)S(1)}, f32[1040,512]{1,0:T(8,128)}, u32[]{:S(2)}) copy-start(f32[1040,512]{1,0:T(8,128)} %get-tuple-element.64) | copy-start | bytes 6389764
  125.1 1.4 copy-start.9
  126.5 1.2 copy-start.17
  133.0 1.6 copy-start.5
  135.4 3.0 %copy-start.28 = (bf16[1040,512]{1,0:T(8,128)(2,1)S(1)}, bf16[1040,512]{1,0:T(8,128)(2,1)}, u32[]{:S(2)}) copy-start(bf16[1040,512]{1,0:T(8,128)(2,1)} %copy-done.27) | copy-start | bytes 3194884
  138.4 1.7 copy-start.48
  141.5 3.2 %copy-start.13 = (bf16[1040,512]{1,0:T(8,128)(2,1)S(1)}, bf16[1040,512]{1,0:T(8,128)(2,1)}, u32[]{:S(2)}) copy-start(bf16[1040,512]{1,0:T(8,128)(2,1)} %copy-done.12) | copy-start | bytes 3194884
  148.2 1.7 copy-start.15
  149.9 2.4 %copy-start.22 = (bf16[1040,512]{1,0:T(8,128)(2,1)S(1)}, bf16[1040,512]{1,0:T(8,128)(2,1)}, u32[]{:S(2)}) copy-start(bf16[1040,512]{1,0:T(8,128)(2,1)} %copy-done.21) | copy-start | bytes 3194884
  152.4 3.1 %copy-start.7 = (bf16[3,512,512]{2,1,0:T(8,128)(2,1)S(1)}, bf16[3,512,512]{2,1,0:T(8,128)(2,1)}, u32[]{:S(2)}) copy-start(bf16[3,512,512]{2,1,0:T(8,128)(2,1)} %copy-done.6) | copy-start | bytes 4718596
  152.4 3.1 %copy-start.18 = (f32[1040,512]{1,0:T(8,128)S(1)}, f32[1040,512]{1,0:T(8,128)}, u32[]{:S(2)}) copy-start(f32[1040,512]{1,0:T(8,128)} %fusion.14) | copy-start | bytes 6389764
  155.5 1.6 copy-start.3
  155.5 3.8 %copy-start.38 = (f32[512,512]{1,0:T(8,128)S(1)}, f32[512,512]{1,0:T(8,128)}, u32[]{:S(2)}) copy-start(f32[512,512]{1,0:T(8,128)} %fusion.49) | copy-start | bytes 3145732
  155.5 3.8 %copy-start.39 = (f32[512,512]{1,0:T(8,128)S(1)}, f32[512,512]{1,0:T(8,128)}, u32[]{:S(2)}) copy-start(f32[512,512]{1,0:T(8,128)} %fusion.35) | copy-start | bytes 3145732
  157.1 2.2 copy-start.31
  157.1 2.2 copy-start.32
  157.1 2.2 copy-start.33
  157.1 3.1 %copy-start.34 = (f32[512,512]{1,0:T(8,128)S(1)}, f32[512,512]{1,0:T(8,128)}, u32[]{:S(2)}) copy-start(f32[512,512]{1,0:T(8,128)} %fusion.41) | copy-start | bytes 3145732
  157.2 3.4 %copy-start.35 = (f32[512,512]{1,0:T(8,128)S(1)}, f32[512,512]{1,0:T(8,128)}, u32[]{:S(2)}) copy-start(f32[512,512]{1,0:T(8,128)} %fusion.43) | copy-start | bytes 3145732
  157.2 3.7 %copy-start.36 = (f32[512,512]{1,0:T(8,128)S(1)}, f32[512,512]{1,0:T(8,128)}, u32[]{:S(2)}) copy-start(f32[512,512]{1,0:T(8,128)} %fusion.45) | copy-start | bytes 3145732
  157.2 3.9 %copy-start.37 = (f32[512,512]{1,0:T(8,128)S(1)}, f32[512,512]{1,0:T(8,128)}, u32[]{:S(2)}) copy-start(f32[512,512]{1,0:T(8,128)} %fusion.47) | copy-start | bytes 3145732
  163.1 2.9 %copy-start.20 = (bf16[130,8,2,128]{3,1,2,0:T(8,128)(2,1)S(1)}, bf16[130,8,2,128]{3,1,2,0:T(8,128)(2,1)}, u32[]{:S(2)}) copy-start(bf16[130,8,2,128]{3,1,2,0:T(8,128)(2,1)} %fusion.96) | copy-start | bytes 1597444
  166.4 1.4 copy-start.40
  166.4 1.7 copy-start.41
  166.5 2.0 copy-start.42
  168.5 2.0 copy-start.43
  170.5 0.6 copy-start.45
  228.3 5.6 %copy-start.1 = (bf16[256,512]{1,0:T(8,128)(2,1)S(1)}, bf16[256,512]{1,0:T(8,128)(2,1)}, u32[]{:S(2)}) copy-start(bf16[256,512]{1,0:T(8,128)(2,1)} %param.17) | copy-start | bytes 786436
